TPU v7x, 512 devices: a whole 4x8x8 slice. The times are simulated.
512 devices in a mesh: seq: 32 (over x, z), tp: 16 (over y, core).
Axes of the slice: x: 4, y: 8, z: 8, core: 2. Of those that a mesh axis runs over, the one named last changes fastest.
Arguments:
- residual: bfloat16 [6144, 8192], P('seq', 'tp'), may hold values from -6 to 6
- attention: bfloat16 [1536, 8192], P('seq'), may hold values from -6 to 6
- quantized_codes: int32 [8192, 8192], P('seq', 'tp'), may hold values from 0 to 15
- absmax: float32 [8192, 128], P('seq', 'tp'), may hold values from 0.005 to 0.05
- adapter_down: bfloat16 [8192, 64], P('seq'), may hold values from -0.0625 to 0.0625
- adapter_up: bfloat16 [64, 8192], P(None, 'tp'), may hold values from -0.75 to 0.75
- routed_slot_gate: float32 [1536], P('seq'), may hold values from 0.2 to 1
- selected: int32 [1536], P('seq'), may hold values from 0 to 191, as said below
- counts: int32 [32], P('seq'), may hold values from 1 to 48, 768 in all
- cotangent: bfloat16 [6144, 8192], P('seq', 'tp'), may hold values from -0.59765625 to 0.59765625
Outputs:
- outgoing_residual: bfloat16 [6144, 8192], P('seq', 'tp')
- attention_output_grad: bfloat16 [1536, 8192], P(None, 'seq')
- adapter_down_gradient: float32 [8192, 64], P('seq')
- adapter_up_gradient: float32 [64, 8192], P(None, 'tp')
- router_gate_gradient: float32 [1536], P('seq')
Inputs may be any that keep to these rules, and one draw needn't show every extreme that they name: `counts`: every shard has at least one live slot, all shards together have 768, and some shard has all 48 slots live. `selected`: within each shard's 48 slots the entries are distinct token positions of that shard; only the first counts entries of a shard are live.
All inputs are finite; a program needn't handle non-finite values.
Results may differ from a plain program's by a relative error of at most 0.0058.
Values may be sent and summed in bfloat16 or wider, within the bound.
A program may use at most 64 MiB of HBM per device.

v0:
```python
import jax
import jax.numpy as jnp
from jax import lax
from jax.sharding import PartitionSpec as P

LEVELS = (
    -1.0,
    -0.6961928009986877,
    -0.5250730514526367,
    -0.39491748809814453,
    -0.28444138169288635,
    -0.18477343022823334,
    -0.09105003625154495,
    0.0,
    0.07958029955625534,
    0.16093020141124725,
    0.24611230194568634,
    0.33791524171829224,
    0.44070982933044434,
    0.5626170039176941,
    0.7229568362236023,
    1.0,
)
adapter_scale = 0.25


def precise_matmul(left, right):
    return jnp.dot(left, right, precision=lax.Precision.HIGHEST, preferred_element_type=jnp.float32)


def dequantize(quantized_codes, absmax):
    quantile_levels = jnp.zeros(quantized_codes.shape, jnp.float32)
    for level_code in range(16):
        quantile_levels = quantile_levels + jnp.where(
            quantized_codes == level_code, LEVELS[level_code], 0.0
        )
    block_size = quantized_codes.shape[1] // absmax.shape[1]
    scales = jnp.repeat(absmax, block_size, axis=1)
    return (quantile_levels * scales).astype(jnp.bfloat16)


def body(
    residual,
    attention,
    quantized_codes,
    absmax,
    adapter_down,
    adapter_up,
    routed_slot_gate,
    selected,
    counts,
    cotangent,
):
    projection_weight = dequantize(quantized_codes, absmax)
    adapter_up_single32 = adapter_up.astype(jnp.float32)
    home_slots = attention.shape[0]
    live_slot = jnp.arange(home_slots, dtype=jnp.int32) < counts[0]
    target = jnp.where(live_slot, selected, residual.shape[0])
    full_w, full_a = (
        lax.all_gather(projection_weight, "seq", axis=0, tiled=True),
        lax.all_gather(adapter_down, "seq", axis=0, tiled=True),
    )
    adapter_product = jnp.dot(attention, full_a, preferred_element_type=jnp.float32)
    block_output = jnp.dot(
        attention, full_w, preferred_element_type=jnp.float32
    ) + adapter_scale * precise_matmul(adapter_product, adapter_up_single32)
    picked = residual[selected].astype(jnp.float32)
    updated = (picked + routed_slot_gate[:, None] * block_output).astype(jnp.bfloat16)
    outgoing_residual = residual.at[target].set(updated, mode="drop")
    upstream = jnp.where(live_slot[:, None], cotangent[selected].astype(jnp.float32), 0.0)
    gate_part = jnp.sum(upstream * block_output, axis=1)
    output_gradient = (routed_slot_gate[:, None] * upstream).astype(jnp.bfloat16)
    head_part = jnp.dot(output_gradient, full_w.T, preferred_element_type=jnp.float32)
    adapter_rank_piece = adapter_scale * jnp.dot(
        output_gradient, adapter_up.T, preferred_element_type=jnp.float32
    )
    head_full, rank_full, router_gate_gradient = lax.psum(
        (head_part, adapter_rank_piece, gate_part), "tp"
    )
    adapter_rank_gradient = rank_full.astype(jnp.bfloat16)
    home_grad = (
        head_full + jnp.dot(adapter_rank_gradient, full_a.T, preferred_element_type=jnp.float32)
    ).astype(jnp.bfloat16)
    attention_output_grad = lax.all_to_all(
        home_grad, "seq", split_axis=1, concat_axis=0, tiled=True
    )
    adapter_down_gradient = lax.psum_scatter(
        jnp.dot(attention.T, adapter_rank_gradient, preferred_element_type=jnp.float32),
        "seq",
        scatter_dimension=0,
        tiled=True,
    )
    up_factor_piece = adapter_scale * precise_matmul(
        adapter_product.T, output_gradient.astype(jnp.float32)
    )
    adapter_up_gradient = lax.psum(up_factor_piece, "seq")
    return (
        outgoing_residual,
        attention_output_grad,
        adapter_down_gradient,
        adapter_up_gradient,
        router_gate_gradient,
    )


def solution(mesh):
    return jax.shard_map(
        body,
        mesh=mesh,
        in_specs=(
            P("seq", "tp"),
            P("seq", None),
            P("seq", "tp"),
            P("seq", "tp"),
            P("seq", None),
            P(None, "tp"),
            P("seq"),
            P("seq"),
            P("seq"),
            P("seq", "tp"),
        ),
        out_specs=(P("seq", "tp"), P(None, "seq"), P("seq", None), P(None, "tp"), P("seq")),
        check_vma=False,
    )
```

profile of v0, /device:TPU:1, one launch (start us, length us, event | category | flops | bytes accessed | tf_op | source)
XLA Modules:
  0.0 710.6 jit_solution(8451295507987079360)
XLA Ops:
  7.2 0.0 all-gather.3.cloned.1.call-start
  7.3 1.3 copy.33
  8.6 2.2 fusion.2
  10.8 0.0 all-gather.3.cloned.1.call-update
  10.8 0.0 all-gather.5.cloned.1.call-start
  10.8 0.7 all-gather.5.cloned.1.call-update
  11.5 0.0 all-reduce.4.cloned.1.call-start
  12.3 0.7 gather_fusion
  13.0 111.5 %all-gather.3.cloned.1.call-done = bf16[8192,512]{0,1:T(8,128)(2,1)} async-done(((bf16[256,512]{0,1:T(8,128)(2,1)}), bf16[8192,512]{0,1:T(8,128)(2,1)}) %all-gather.3.cloned.1.call-update) | async-done | bytes 8388624 | tf_op jit(solution)/shard_map/all_gather | solution.py:60
  124.4 6.1 fusion.8
  130.6 0.0 all-reduce.4.cloned.1.call-update
  130.6 0.0 all-reduce.6.cloned.1.call-start
  130.7 0.2 convolution_multiply_fusion.2
  130.9 69.4 %all-gather.5.cloned.1.call-done = bf16[8192,64]{0,1:T(8,128)(2,1)} async-done(((bf16[256,64]{0,1:T(8,128)(2,1)}), bf16[8192,64]{0,1:T(8,128)(2,1)}) %all-gather.5.cloned.1.call-update) | async-done | bytes 1048592 | tf_op jit(solution)/shard_map/all_gather | solution.py:61
  200.3 1.6 fusion.9
  201.9 0.9 convolution_multiply_fusion
  202.9 0.0 reduce-scatter.2.cloned.1.call-start
  202.9 6.0 convolution_bitcast_fusion.1
  208.9 0.3 multiply_reduce_fusion
  209.2 47.0 %all-reduce = (bf16[48,64]{1,0:T(8,128)(2,1)S(1)}, f32[48]{0:T(128)}) all-reduce(f32[48,64]{1,0:T(8,128)S(1)} %convolution_multiply_fusion.2, f32[48]{0:T(128)S(1)} %get-tuple-element.9), channel_id=1, replica_groups=mesh['seq'=32,'tp'=16] {'tp'}, use_global_device_ids=true, to_apply=%region_2.3 | all-reduce | flops 3120 | bytes 18816 | tf_op jit(solution)/shard_map/psum | solution.py:77
  256.3 1.8 convolution_bitcast_fusion
  258.1 0.0 reduce-scatter.2.cloned.1.call-update
  258.1 65.5 %all-reduce.4.cloned.1.call-done = f32[48,8192]{1,0:T(8,128)} async-done(((f32[48,8192]{1,0:T(8,128)}), f32[48,8192]{1,0:T(8,128)}) %all-reduce.4.cloned.1.call-update) | async-done | bytes 1572880 | tf_op jit(solution)/shard_map/psum | solution.py:77
  323.6 1.8 fusion
  325.4 0.9 copy.51
  326.3 9.9 %all-to-all-start = ((bf16[48,32,256]{2,0,1:T(8,128)(2,1)}), bf16[48,32,256]{2,0,1:T(8,128)(2,1)S(1)}, u32[]{:S(2)}, u32[]{:S(2)}) async-start(bf16[48,32,256]{2,0,1:T(8,128)(2,1)} %bitcast.28), calls=%async_computation | async-start | bytes 1572864 | tf_op jit(solution)/shard_map/all_to_all | solution.py:84
  336.2 1.2 scatter_custom_fusion
  337.4 18.9 %all-to-all-done = bf16[48,32,256]{2,0,1:T(8,128)(2,1)S(1)} async-done(((bf16[48,32,256]{2,0,1:T(8,128)(2,1)}), bf16[48,32,256]{2,0,1:T(8,128)(2,1)S(1)}, u32[]{:S(2)}, u32[]{:S(2)}) %all-to-all-start) | async-done | bytes 786464 | tf_op jit(solution)/shard_map/all_to_all | solution.py:84
  356.4 121.5 %all-reduce.6.cloned.1.call-done = f32[64,512]{1,0:T(8,128)} async-done(((f32[64,512]{1,0:T(8,128)}), f32[64,512]{1,0:T(8,128)}) %all-reduce.6.cloned.1.call-update) | async-done | bytes 131088 | tf_op jit(solution)/shard_map/psum | solution.py:96
  477.8 223.8 %reduce-scatter.2.cloned.1.call-done = f32[256,64]{0,1:T(8,128)} async-done(((f32[8192,64]{0,1:T(8,128)}), f32[256,64]{0,1:T(8,128)}) %reduce-scatter.2.cloned.1.call-update) | async-done | bytes 65552 | tf_op jit(solution)/shard_map/reduce_scatter | solution.py:87
  701.6 0.9 copy.59
  702.5 1.6 copy.60
  (20 shorter events, 0.1 us)
Async XLA Ops:
  7.2 193.1 %copy-start = (bf16[48,8192]{1,0:T(8,128)(2,1)S(1)}, bf16[48,8192]{1,0:T(8,128)(2,1)}, u32[]{:S(2)}) copy-start(bf16[48,8192]{1,0:T(8,128)(2,1)} %param.11) | copy-start | bytes 2359300
  7.2 5.1 copy-start.7
  7.2 5.1 copy-start.4
  7.2 117.2 %copy-start.6 = (f32[48]{0:T(128)S(1)}, f32[48]{0:T(128)}, u32[]{:S(2)}) copy-start(f32[48]{0:T(128)} %param.16) | copy-start | bytes 580
  7.2 117.2 %all-gather.3.cloned.1.call-start = ((), (), s32[]{:S(2)}) async-start(), calls=%async_computation.2 | async-start | bytes 8650752 | tf_op jit(solution)/shard_map/all_gather | solution.py:60
  10.8 189.5 %all-gather.5.cloned.1.call-start = ((), (), s32[]{:S(2)}) async-start(), calls=%async_computation.3 | async-start | bytes 1081344 | tf_op jit(solution)/shard_map/all_gather | solution.py:61
  11.5 312.1 %all-reduce.4.cloned.1.call-start = ((), (), s32[]{:S(2)}) async-start(), calls=%async_computation.4 | async-start | bytes 3145728 | tf_op jit(solution)/shard_map/psum | solution.py:77
  13.0 117.7 %copy-start.5 = (bf16[64,512]{1,0:T(8,128)(2,1)S(1)}, bf16[64,512]{1,0:T(8,128)(2,1)}, u32[]{:S(2)}) copy-start(bf16[64,512]{1,0:T(8,128)(2,1)} %param.15) | copy-start | bytes 196612
  130.6 347.2 %all-reduce.6.cloned.1.call-start = ((), (), s32[]{:S(2)}) async-start(), calls=%async_computation.6 | async-start | bytes 262144 | tf_op jit(solution)/shard_map/psum | solution.py:96
  202.9 498.7 %reduce-scatter.2.cloned.1.call-start = ((), (), s32[]{:S(2)}) async-start(), calls=%async_computation.5 | async-start | bytes 2162688 | tf_op jit(solution)/shard_map/reduce_scatter | solution.py:87
  256.3 67.3 %copy-start.1 = (bf16[8192,64]{0,1:T(8,128)(2,1)S(1)}, bf16[8192,64]{0,1:T(8,128)(2,1)}, u32[]{:S(2)}) copy-start(bf16[8192,64]{0,1:T(8,128)(2,1)} %all-gather.5.cloned.1.call-done) | copy-start | bytes 3145732
  325.4 10.9 %copy-start.3 = (bf16[192,512]{1,0:T(8,128)(2,1)S(1)}, bf16[192,512]{1,0:T(8,128)(2,1)}, u32[]{:S(2)}) copy-start(bf16[192,512]{1,0:T(8,128)(2,1)} %param.10) | copy-start | bytes 589828
  326.3 30.0 %all-to-all-start = ((bf16[48,32,256]{2,0,1:T(8,128)(2,1)}), bf16[48,32,256]{2,0,1:T(8,128)(2,1)S(1)}, u32[]{:S(2)}, u32[]{:S(2)}) async-start(bf16[48,32,256]{2,0,1:T(8,128)(2,1)} %bitcast.28), calls=%async_computation | async-start | bytes 1572864 | tf_op jit(solution)/shard_map/all_to_all | solution.py:84
  337.4 366.6 %copy-start.2 = (bf16[192,512]{1,0:T(8,128)(2,1)}, bf16[192,512]{1,0:T(8,128)(2,1)S(1)}, u32[]{:S(2)}) copy-start(bf16[192,512]{1,0:T(8,128)(2,1)S(1)} %scatter_custom_fusion) | copy-start | bytes 589828
Sparse Core Ops, SparseCore 0:
  11.7 112.7 all-gather.2
  127.5 72.7 all-gather.4
  202.6 120.9 all-reduce.3
  327.9 149.8 all-reduce.5
  482.6 218.8 reduce-scatter.1
where the time goes:
time: 715 us; the launch traced here: 711 us
  waiting for transfers between devices  611 us (85%)
  blocking collectives  47 us (7%)
  matrix products  18.8 us (3%)
  between operations  14.6 us (2%)
  starting transfers between devices  10.1 us (1%)
    reduce_scatter x1, waiting for transfers between devices, body(): lax.psum_scatter(jnp.dot(attention.T, adapter_rank_gradient, preferred_el...  224 us
    psum x1, waiting for transfers between devices, body(): adapter_up_gradient = lax.psum(up_factor_piece, 'seq')  121 us
    all_gather x1, waiting for transfers between devices, body(): lax.all_gather(projection_weight, 'seq', axis=0, tiled=True)  111 us
    all_gather x1, waiting for transfers between devices, body(): lax.all_gather(adapter_down, 'seq', axis=0, tiled=True)  69.4 us
    psum x1, waiting for transfers between devices, body(): lax.psum((head_part, adapter_rank_piece, gate_part), 'tp')  65.5 us
    psum x1, blocking collectives, body(): lax.psum((head_part, adapter_rank_piece, gate_part), 'tp')  47 us
    all_to_all x1, waiting for transfers between devices, body(): lax.all_to_all(home_grad, 'seq', split_axis=1, concat_axis=0, tiled=True)  18.9 us
  transfers between devices with their start and end apart: 6, of which 6 were waited for; matrix products, arithmetic and copies ran while one was open for 3% of the time, Pallas kernels for 0%

commit v1 on v0

v1 whole, which is shorter than its diff:
```python
import functools

import jax
import jax.numpy as jnp
from jax import lax
from jax.experimental import pallas as pl
from jax.experimental.pallas import tpu as pltpu
from jax.sharding import PartitionSpec as P

LEVELS = (
    -1.0,
    -0.6961928009986877,
    -0.5250730514526367,
    -0.39491748809814453,
    -0.28444138169288635,
    -0.18477343022823334,
    -0.09105003625154495,
    0.0,
    0.07958029955625534,
    0.16093020141124725,
    0.24611230194568634,
    0.33791524171829224,
    0.44070982933044434,
    0.5626170039176941,
    0.7229568362236023,
    1.0,
)
adapter_scale = 0.25
F32, BF16 = jnp.float32, jnp.bfloat16
MESH = pl.DeviceIdType.MESH

NX, NZ, NY, NC = 4, 8, 8, 2

(S_G, S_W, S_DT, S_A, S_ASIB, S_RSIB, S_RRS, S_RAG, S_HSIB, S_HRS, S_FX, S_FY, S_FSIB,
 S_URS, S_UX, S_UAG, S_ORS, S_DX, S_GG, S_FX2, N_SEM) = range(21)
(L_COT, L_CODES, L_ABS, L_DOWN, L_UP, L_RES, L_A, L_FOUT, L_OUT, L_D, L_U, N_LOC) = range(12)


def dot(a, b, ca, cb):
    return lax.dot_general(a, b, (((ca,), (cb,)), ((), ())), preferred_element_type=F32)


def split(value):
    high = value.astype(BF16)
    return high, (value - high.astype(F32)).astype(BF16)


def to_column(row, n):
    at = lax.broadcasted_iota(jnp.int32, (n, n), 0) == lax.broadcasted_iota(jnp.int32, (n, n), 1)
    return jnp.sum(jnp.where(at, jnp.broadcast_to(row, (n, n)), 0.0), axis=1, keepdims=True)


def to_row(column, n):
    at = lax.broadcasted_iota(jnp.int32, (n, n), 0) == lax.broadcasted_iota(jnp.int32, (n, n), 1)
    return jnp.sum(jnp.where(at, jnp.broadcast_to(column, (n, n)), 0.0), axis=0, keepdims=True)


def kernel(nx, nz, ny,
           res_hbm, attn, codes_hbm, abs_hbm, down_hbm, up_hbm, gate_ref, sel_ref, counts_ref, cot_hbm,
           out_res, out_ag, out_d, out_u, out_gate,
           res, codes, absm, up, cot, scales,
           a_all, w_all, dt_all, g_all,
           rt, rt_sib, rt_send, rt_recv, rag_send, rag,
           h_send, h_sib, hs, hr, f_send, fx,
           u_send, u_recv, ux_send, ux_recv, uag,
           o_send, o_recv, o_home, new_res,
           d_send, d_recv, d_new, u_new, gg_send, gg_recv,
           ssem, rsem, lsem):
    tokens, cols = res.shape
    heads = w_all.shape[1]
    cap = gate_ref.shape[1]
    rank = up.shape[0]
    slots = nz * cap
    hx = nx // NC
    ntp = ny * NC

    seq = lax.axis_index("seq")
    tp = lax.axis_index("tp")
    x, z = seq // nz, seq % nz
    y, c = tp // NC, tp % NC

    def dev_x(k):
        return (((x + k) % nx) * nz + z, tp)

    def dev_z(k):
        return (x * nz + (z + k) % nz, tp)

    def dev_y(k):
        return (seq, ((y + k) % ny) * NC + c)

    def dev_tp(k):
        return (seq, (tp + k) % ntp)

    sibling = (seq, y * NC + (1 - c))

    def send(group, src, dst, device):
        pltpu.make_async_remote_copy(
            src_ref=src, dst_ref=dst, send_sem=ssem.at[group], recv_sem=rsem.at[group],
            device_id=device, device_id_type=MESH,
        ).start()

    def take(group, like):
        pltpu.make_async_copy(like, like, rsem.at[group]).wait()

    def sent(group, like):
        pltpu.make_async_copy(like, like, ssem.at[group]).wait()

    def local(which, src, dst):
        copy = pltpu.make_async_copy(src, dst, lsem.at[which])
        copy.start()
        return copy

    cot_in = local(L_COT, cot_hbm, cot)
    codes_in = local(L_CODES, codes_hbm, codes)
    abs_in = local(L_ABS, abs_hbm, absm)
    down_in = local(L_DOWN, down_hbm, dt_all.at[0])
    up_in = local(L_UP, up_hbm, up)
    res_in = local(L_RES, res_hbm, res)

    barrier = pltpu.get_barrier_semaphore()
    for k in range(1, nx):
        pl.semaphore_signal(barrier, inc=1, device_id=dev_x(k), device_id_type=MESH)
    for k in range(1, nz):
        pl.semaphore_signal(barrier, inc=1, device_id=dev_z(k), device_id_type=MESH)
    for k in range(1, ntp):
        pl.semaphore_signal(barrier, inc=1, device_id=dev_tp(k), device_id_type=MESH)

    for i in range(nx):
        at = pl.multiple_of((((x + i) % nx) * nz + z) * heads, heads)
        local(L_A, attn.at[:, pl.ds(at, heads)], a_all.at[i, pl.ds(0, cap)])

    gate = to_column(gate_ref[...], cap)
    picked_token = to_column(sel_ref[...].astype(F32), cap)
    live = lax.broadcasted_iota(jnp.int32, (cap, tokens), 0) < counts_ref[...]
    pick = jnp.where(
        live & (lax.broadcasted_iota(jnp.int32, (cap, tokens), 1).astype(F32) == picked_token), 1.0, 0.0)
    pick_bf = pick.astype(BF16)
    cot_in.wait()
    upstream = dot(pick_bf, cot[...], 1, 0)
    g_all[pl.ds(0, cap), :] = (gate * upstream).astype(BF16)

    codes_in.wait()
    abs_in.wait()
    step = 32

    scale_high = absm[...].astype(BF16)
    rest = absm[...] - scale_high.astype(F32)
    scale_mid, scale_low = split(rest)
    qblocks = absm.shape[0]
    spread_to = jnp.where(
        lax.broadcasted_iota(jnp.int32, (qblocks, cols), 1) // (cols // qblocks)
        == lax.broadcasted_iota(jnp.int32, (qblocks, cols), 0), 1.0, 0.0).astype(BF16)
    scales[...] = (dot(scale_high, spread_to, 0, 0) + dot(scale_mid, spread_to, 0, 0)
                   + dot(scale_low, spread_to, 0, 0))

    def dequantize(n, carry):
        rows = pl.ds(pl.multiple_of(n * step, step), step)
        for q in range(cols // 128):
            code = codes[rows, pl.ds(q * 128, 128)]
            b0, b1, b2, b3 = [(code & (1 << bit)) != 0 for bit in range(4)]
            level = LEVELS
            for bit in (b0, b1, b2, b3):
                level = [jnp.where(bit, level[m + 1], level[m]) for m in range(0, len(level), 2)]
            scale = scales[rows, pl.ds(q * 128, 128)]
            w_all[0, rows, pl.ds(q * 128, 128)] = (level[0] * scale).astype(BF16)
        return carry

    lax.fori_loop(0, heads // step, dequantize, 0)
    down_in.wait()

    pl.semaphore_wait(barrier, (nx - 1) + (nz - 1) + (ntp - 1))

    for k in range(1, nz):
        send(S_G, g_all.at[pl.ds(0, cap)], g_all.at[pl.ds(cap * (nz - k), cap)], dev_z(k))
    for k in range(1, nx):
        send(S_W, w_all.at[0], w_all.at[nx - k], dev_x(k))
        send(S_DT, dt_all.at[0], dt_all.at[nx - k], dev_x(k))
    for k in range(1, nz):
        for n in range(hx):
            i = hx * c + n
            at = pl.multiple_of((((x + i) % nx) * nz + (z + k) % nz) * heads, heads)
            send(S_A, attn.at[:, pl.ds(at, heads)],
                 a_all.at[i, pl.ds(cap * (nz - k), cap)], dev_z(k))

    g_rest = g_all.at[pl.ds(cap, slots - cap)]
    w_rest = w_all.at[pl.ds(1, nx - 1)]
    dt_rest = dt_all.at[pl.ds(1, nx - 1)]
    a_mine = a_all.at[pl.ds(hx * c, hx), pl.ds(cap, slots - cap)]
    a_other = a_all.at[pl.ds(hx * (1 - c), hx), pl.ds(cap, slots - cap)]

    up_in.wait()
    take(S_G, g_rest)
    rt[...] = adapter_scale * dot(up[...], g_all[...], 1, 1)
    send(S_RSIB, rt, rt_sib, sibling)
    rank_part = (adapter_scale * dot(g_all[...], up[...], 1, 1)).astype(BF16)

    take(S_W, w_rest)
    take(S_DT, dt_rest)
    for i in range(nx):
        part = dot(g_all[...], w_all[i], 1, 1) + dot(rank_part, dt_all[i], 1, 0)
        for j in range(nz):
            h_send[i // hx, j, i % hx] = part[j * cap:(j + 1) * cap].astype(BF16)
    send(S_HSIB, h_send.at[1 - c], h_sib, sibling)

    take(S_RSIB, rt_sib)
    for j in range(ny):
        rows = pl.ds(j * (rank // ny), rank // ny)
        rt_send[j] = rt[rows, :] + rt_sib[rows, :]
    for k in range(1, ny):
        send(S_RRS, rt_send.at[(y + k) % ny], rt_recv.at[ny - k], dev_y(k))

    take(S_HSIB, h_sib)
    for j in range(nz):
        hs[j] = (h_send[c, j].astype(F32) + h_sib[j].astype(F32)).astype(BF16)
    for k in range(1, ny):
        send(S_HRS, hs.at[(y + k) % ny], hr.at[ny - k], dev_y(k))

    take(S_RRS, rt_recv.at[pl.ds(1, ny - 1)])
    total = rt_send[y]
    for k in range(1, ny):
        total = total + rt_recv[k]
    rag_send[...] = total.astype(BF16).astype(F32)
    rag[y] = rag_send[...]
    for k in range(1, ny):
        send(S_RAG, rag_send, rag.at[y], dev_y(k))

    take(S_A, a_mine)
    send(S_ASIB, a_mine, a_mine, sibling)
    a_home = a_all.at[:, pl.ds(0, cap)]
    pltpu.make_async_copy(a_home, a_home, lsem.at[L_A]).wait()
    take(S_ASIB, a_other)

    low = jnp.zeros((slots, rank), F32)
    low_t = jnp.zeros((rank, slots), F32)
    for i in range(nx):
        low = low + dot(a_all[i], dt_all[i], 1, 1)
        low_t = low_t + dot(dt_all[i], a_all[i], 1, 1)
    t_high, t_low = split(low_t)
    part = adapter_scale * (dot(t_high, g_all[...], 1, 0) + dot(t_low, g_all[...], 1, 0))
    for j in range(nz):
        u_send[j] = part[j * (rank // nz):(j + 1) * (rank // nz)]
    for k in range(1, nz):
        send(S_URS, u_send.at[(z + k) % nz], u_recv.at[nz - k], dev_z(k))

    high, small = split(adapter_scale * low)
    part = dot(high, up[...], 1, 0) + dot(small, up[...], 1, 0)
    for i in range(nx):
        part = part + dot(a_all[i], w_all[i], 1, 0)
    o_home[...] = part[:cap]
    for j in range(1, nz):
        o_send[j] = part[j * cap:(j + 1) * cap].astype(BF16)
    for k in range(1, nz):
        send(S_ORS, o_send.at[k], o_recv.at[nz - k], dev_z(k))

    take(S_HRS, hr.at[pl.ds(1, ny - 1)])
    total = hs[y].astype(F32)
    for k in range(1, ny):
        total = total + hr[k].astype(F32)
    f_send[...] = total.astype(BF16)
    shard_z = (z + y) % nz
    for n in range(hx):
        i = hx * c + n
        if n == 0:
            @pl.when(c == 0)
            def _():
                fx[0] = f_send[0]

            @pl.when(c != 0)
            def _():
                send(S_FX, f_send.at[0], fx.at[0], dev_x(hx))
        else:
            send(S_FX2 + n - 1, f_send.at[n], fx.at[n], dev_x(i))

    take(S_RAG, rag.at[pl.ds(0, ny - 1)])
    full_rt = jnp.reshape(rag[...], (rank, slots)).astype(BF16)
    for i in range(nx):
        d_send[i] = dot(full_rt, a_all[i], 1, 0)
    for k in range(1, nx):
        send(S_DX, d_send.at[k], d_recv.at[nx - k], dev_x(k))

    for n in range(hx):
        if n == 0:
            @pl.when(c != 0)
            def _():
                take(S_FX, fx.at[0])
        else:
            take(S_FX2 + n - 1, fx.at[n])
    for n in range(hx):
        row = (x + nx - (hx * c + n)) % nx
        local(L_FOUT, fx.at[n], out_ag.at[row, shard_z])
        for k in range(1, ny):
            send(S_FY, fx.at[n], out_ag.at[row, shard_z], dev_y(k))

    take(S_URS, u_recv.at[pl.ds(1, nz - 1)])
    total = u_send[z]
    for k in range(1, nz):
        total = total + u_recv[k]
    ux_send[...] = total
    for k in range(1, nx):
        send(S_UX, ux_send, ux_recv.at[nx - k], dev_x(k))

    take(S_ORS, o_recv.at[pl.ds(1, nz - 1)])
    block = o_home[...]
    for k in range(1, nz):
        block = block + o_recv[k].astype(F32)
    res_in.wait()
    gate_part = to_row(jnp.sum(upstream * block, axis=1, keepdims=True), cap)
    gg_send[...] = jnp.zeros_like(gg_send)
    gg_send[:, pl.ds(0, cap)] = jnp.broadcast_to(gate_part, (8, cap))
    for k in range(1, ntp):
        send(S_GG, gg_send, gg_recv.at[ntp - k], dev_tp(k))
    picked = dot(pick_bf, res[...], 1, 0)
    updated = (picked + gate * block).astype(BF16)
    spread = dot(pick_bf, updated, 0, 0)
    taken = dot(pick_bf, jnp.ones((cap, 128), BF16), 0, 0)[:, :1] > 0.5
    new_res[...] = jnp.where(taken, spread, res[...].astype(F32)).astype(BF16)
    out_copy = local(L_OUT, new_res, out_res)

    take(S_UX, ux_recv.at[pl.ds(1, nx - 1)])
    total = ux_send[...]
    for k in range(1, nx):
        total = total + ux_recv[k]
    ux_send_sum = total
    sent(S_UX, ux_recv.at[pl.ds(1, nx - 1)])
    ux_send[...] = ux_send_sum
    uag[z] = ux_send_sum
    for k in range(1, nz):
        send(S_UAG, ux_send, uag.at[z], dev_z(k))

    take(S_DX, d_recv.at[pl.ds(1, nx - 1)])
    total = d_send[0]
    for k in range(1, nx):
        total = total + d_recv[k]
    d_new[...] = total
    d_copy = local(L_D, d_new, out_d)

    take(S_FY, out_ag.at[pl.ds(0, hx), pl.ds(0, ny - 1)])
    pltpu.make_async_copy(fx, fx, lsem.at[L_FOUT]).wait()
    for n in range(hx):
        row = (x + nx - (hx * c + n)) % nx
        send(S_FSIB, out_ag.at[row], out_ag.at[row], sibling)

    take(S_GG, gg_recv.at[pl.ds(1, ntp - 1)])
    total = gg_send[...]
    for k in range(1, ntp):
        total = total + gg_recv[k]
    out_gate[...] = total[:1, :cap]

    take(S_UAG, uag.at[pl.ds(0, nz - 1)])
    u_new[...] = jnp.reshape(uag[...], (rank, cols))
    u_copy = local(L_U, u_new, out_u)
    take(S_FSIB, out_ag.at[pl.ds(0, hx)])

    out_copy.wait()
    d_copy.wait()
    u_copy.wait()
    sent(S_G, g_rest)
    sent(S_W, w_rest)
    sent(S_DT, dt_rest)
    sent(S_A, a_mine)
    sent(S_ASIB, a_mine)
    sent(S_RSIB, rt)
    sent(S_RRS, rt_recv.at[pl.ds(1, ny - 1)])
    sent(S_RAG, rag.at[pl.ds(0, ny - 1)])
    sent(S_HSIB, h_sib)
    sent(S_HRS, hr.at[pl.ds(1, ny - 1)])
    for n in range(hx):
        if n == 0:
            @pl.when(c != 0)
            def _():
                sent(S_FX, fx.at[0])
        else:
            sent(S_FX2 + n - 1, fx.at[n])
    sent(S_FY, out_ag.at[pl.ds(0, hx), pl.ds(0, ny - 1)])
    sent(S_FSIB, out_ag.at[pl.ds(0, hx)])
    sent(S_URS, u_recv.at[pl.ds(1, nz - 1)])
    sent(S_UAG, uag.at[pl.ds(0, nz - 1)])
    sent(S_ORS, o_recv.at[pl.ds(1, nz - 1)])
    sent(S_DX, d_recv.at[pl.ds(1, nx - 1)])
    sent(S_GG, gg_recv.at[pl.ds(1, ntp - 1)])


def body(residual, attention, codes, absmax, down, up, gate, selected, counts, cotangent,
         nx=NX, nz=NZ, ny=NY):
    tokens, cols = residual.shape
    cap = attention.shape[0]
    heads, rank = down.shape
    slots = nz * cap
    hx = nx // NC
    ntp = ny * NC
    anywhere = pl.BlockSpec(memory_space=pl.ANY)
    vmem = pl.BlockSpec(memory_space=pltpu.VMEM)

    def f32(*shape):
        return pltpu.VMEM(shape, F32)

    def bf16(*shape):
        return pltpu.VMEM(shape, BF16)

    outs = pl.pallas_call(
        functools.partial(kernel, nx, nz, ny),
        out_shape=(
            jax.ShapeDtypeStruct((tokens, cols), BF16),
            jax.ShapeDtypeStruct((nx, nz, cap, heads), BF16),
            jax.ShapeDtypeStruct((rank, heads), F32),
            jax.ShapeDtypeStruct((rank, cols), F32),
            jax.ShapeDtypeStruct((1, cap), F32),
        ),
        in_specs=[anywhere] * 6 + [vmem, vmem, vmem, anywhere],
        out_specs=(anywhere, anywhere, anywhere, anywhere, vmem),
        scratch_shapes=[
            bf16(tokens, cols), pltpu.VMEM((heads, cols), jnp.int32), f32(*absmax.shape[::-1]),
            bf16(rank, cols), bf16(tokens, cols), f32(heads, cols),
            bf16(nx, slots, heads), bf16(nx, heads, cols), bf16(nx, rank, heads), bf16(slots, cols),
            f32(rank, slots), f32(rank, slots), f32(ny, rank // ny, slots), f32(ny, rank // ny, slots),
            f32(rank // ny, slots), f32(ny, rank // ny, slots),
            bf16(NC, nz, hx, cap, heads), bf16(nz, hx, cap, heads), bf16(nz, hx, cap, heads),
            bf16(ny, hx, cap, heads), bf16(hx, cap, heads), bf16(hx, cap, heads),
            f32(nz, rank // nz, cols), f32(nz, rank // nz, cols), f32(rank // nz, cols),
            f32(nx, rank // nz, cols), f32(nz, rank // nz, cols),
            bf16(nz, cap, cols), bf16(nz, cap, cols), f32(cap, cols), bf16(tokens, cols),
            f32(nx, rank, heads), f32(nx, rank, heads), f32(rank, heads), f32(rank, cols),
            f32(8, 128), f32(ntp, 8, 128),
            pltpu.SemaphoreType.DMA((N_SEM,)), pltpu.SemaphoreType.DMA((N_SEM,)),
            pltpu.SemaphoreType.DMA((N_LOC,)),
        ],
        compiler_params=pltpu.CompilerParams(
            collective_id=0, has_side_effects=True, vmem_limit_bytes=56 << 20),
        name="block_step",
    )(residual, attention, codes, absmax.T, down.T, up, gate.reshape(1, cap), selected.reshape(1, cap),
      counts.reshape(1, 1), cotangent)
    new_res, head_grad, d_grad, u_grad, g_grad = outs
    return new_res, head_grad.reshape(nx * nz * cap, heads), d_grad.T, u_grad, g_grad.reshape(cap)


def solution(mesh):
    return jax.shard_map(
        body,
        mesh=mesh,
        in_specs=(
            P("seq", "tp"),
            P("seq", None),
            P("seq", "tp"),
            P("seq", "tp"),
            P("seq", None),
            P(None, "tp"),
            P("seq"),
            P("seq"),
            P("seq"),
            P("seq", "tp"),
        ),
        out_specs=(P("seq", "tp"), P(None, "seq"), P("seq", None), P(None, "tp"), P("seq")),
        check_vma=False,
    )
```

time: 715 us -> 69.3 us (0.10)
  waiting for transfers between devices: 611 us -> 0 us
  Pallas kernels: 0 us -> 61.5 us
  blocking collectives: 47 us -> 0 us
  matrix products: 18.8 us -> 0 us
  between operations: 14.6 us -> 1.29 us
  starting transfers between devices: 10.1 us -> 0 us
    reduce_scatter x1 -> x0, waiting for transfers between devices: 224 us -> none  [body(): lax.psum_scatter(jnp.dot(attention.T, adapter_rank_gradient, preferred_el...]
    psum x2 -> x0, waiting for transfers between devices: 187 us -> none  [the longest x1 121 us: body(): adapter_up_gradient = lax.psum(up_factor_piece, 'seq')]
    all_gather x2 -> x0, waiting for transfers between devices: 181 us -> none  [the longest x1 111 us: body(): lax.all_gather(projection_weight, 'seq', axis=0, tiled=True)]
    pallas_call x0 -> x1, Pallas kernels: none -> 61.5 us  [body(): pl.pallas_call(functools.partial(kernel, nx, nz, ny), out_shape=(jax.Shap...]
    psum x1 -> x0, blocking collectives: 47 us -> none  [body(): lax.psum((head_part, adapter_rank_piece, gate_part), 'tp')]
    all_to_all x1 -> x0, waiting for transfers between devices: 18.9 us -> none  [body(): lax.all_to_all(home_grad, 'seq', split_axis=1, concat_axis=0, tiled=True)]
    dot_general x8 -> x0, matrix products: 18.8 us -> none  [the longest x1 6.14 us: body(): jnp.dot(output_gradient, full_w.T, preferred_element_type=jnp.float32)]
    all_to_all x1 -> x0, starting transfers between devices: 9.9 us -> none  [body(): lax.all_to_all(home_grad, 'seq', split_axis=1, concat_axis=0, tiled=True)]
  transfers between devices with their start and end apart: 6 -> 0, of which waited for: 6 -> 0; matrix products, arithmetic and copies ran while one was open for 3% -> 0% of each run, Pallas kernels for 0% -> 0%
where the time goes in v1:
time: 69.3 us; the launch traced here: 68.6 us
  Pallas kernels  61.5 us (89%)
  local copies, waits for them, and re-layouts  5.81 us (8%)
  between operations  1.29 us (2%)
    pallas_call x1, Pallas kernels, body(): pl.pallas_call(functools.partial(kernel, nx, nz, ny), out_shape=(jax.Shap...  61.5 us
    unnamed x11, local copies, waits for them, and re-layouts  5.81 us

profile of v1, /device:TPU:1, one launch (start us, length us, event | category | flops | bytes accessed | tf_op | source)
XLA Modules:
  0.0 68.6 jit_solution(1931449529553226625)
XLA Ops:
  1.3 61.5 %block_step.1 = (bf16[192,512]{1,0:T(8,128)(2,1)}, bf16[4,8,48,256]{3,2,1,0:T(8,128)(2,1)}, f32[64,256]{1,0:T(8,128)}, f32[64,512]{1,0:T(8,128)}, f32[1,48]{1,0:T(1,128)}) custom-call(bf16[192,512]{1,0:T(8,128)(2,1)} %res_hbm.1, bf16[48,8192]{1,0:T(8,128)(2,1)} %attn.1, s32[256,512]{1,0:T(8,128)} %codes_hbm.1, f32[8,256]{1,0:T(8,128)} %bitcast.12, ...), custom_call_target="tpu_custom_call" | custom-call | tf_op jit(solution)/shard_map/block_step/pallas_call | solution.py:400
  62.8 1.6 %copy.21 = bf16[192,512]{1,0:T(8,128)(2,1)} copy(bf16[192,512]{1,0:T(8,128)(2,1)} %get-tuple-element.20) | data formatting | bytes 393216
  64.4 0.0 copy-start.1
  64.4 2.1 %copy.22 = bf16[1536,256]{1,0:T(8,128)(2,1)} copy(bf16[1536,256]{1,0:T(8,128)(2,1)} %bitcast.9) | data formatting | bytes 1572864
  66.5 0.0 copy-done.1
  66.5 0.0 copy-start
  66.5 0.6 copy.23
  67.1 0.3 copy-done
  67.4 0.0 copy-start.2
  67.4 0.7 copy.24
  68.1 0.0 copy-done.2
  68.1 0.5 copy.25
Async XLA Ops:
  64.4 2.1 %copy-start.1 = (f32[64,256]{1,0:T(8,128)S(1)}, f32[64,256]{1,0:T(8,128)}, u32[]{:S(2)}) copy-start(f32[64,256]{1,0:T(8,128)} %get-tuple-element.12) | copy-start | bytes 196612
  66.5 0.9 %copy-start = (f32[64,512]{1,0:T(8,128)S(1)}, f32[64,512]{1,0:T(8,128)}, u32[]{:S(2)}) copy-start(f32[64,512]{1,0:T(8,128)} %get-tuple-element.23) | copy-start | bytes 393220
  67.4 0.7 copy-start.2

commit v2 on v1

--- a/solution.py
+++ b/solution.py
@@ -31,9 +31,10 @@
 
 NX, NZ, NY, NC = 4, 8, 8, 2
 
-(S_G, S_W, S_DT, S_A, S_ASIB, S_RSIB, S_RRS, S_RAG, S_HSIB, S_HRS, S_FX, S_FY, S_FSIB,
- S_URS, S_UX, S_UAG, S_ORS, S_DX, S_GG, S_FX2, N_SEM) = range(21)
-(L_COT, L_CODES, L_ABS, L_DOWN, L_UP, L_RES, L_A, L_FOUT, L_OUT, L_D, L_U, N_LOC) = range(12)
+(S_G, S_A, S_F0, S_F1, S_AZ, S_W1A, S_W1B, S_W3A, S_W3B, S_W2, S_DT, S_ASIB, S_RSIB, S_RRS, S_RAG,
+ S_HSIB, S_HRS, S_FX, S_FSIB, S_URS, S_UX, S_UAG, S_ORS, S_DX, S_GG, N_SEM) = (
+    0, 5, 10, 15, 20, *range(22, 32), 32, 34, 36, 38, *range(40, 47))
+(L_COT, L_CODES, L_ABS, L_DOWN, L_UP, L_RES, L_A, L_OUT, L_D, L_U, L_FOUT, N_LOC) = (*range(11), 12)
 
 
 def dot(a, b, ca, cb):
@@ -110,6 +111,79 @@
         copy.start()
         return copy
 
+    def gather_start(group, n, dev, parts):
+        for k in sorted({1, n - 1} | ({2, n - 2} if n == 8 else set())):
+            which = {n - 1: 0, 1: 1, n - 2: 2, 2: 3}[n - k] if n > 2 else 0
+            for src, dst in zip(parts(0, 0), parts(0, k)):
+                send(group + which, src, dst, dev(k))
+
+    def gather_forward(group, n, dev, parts, halves, like):
+        if n == 2:
+            return
+        far = n // 2 - 2
+        for side, which in ((-1, 2 if far else 0), (1, 3 if far else 1)):
+            j = side * (far if far else 1)
+            take(group + which, like(1))
+            if far:
+                for src, dst in zip(parts(j, 0), parts(j, -side)):
+                    send(group + 4, src, dst, dev(-side))
+            half = 0 if side < 0 else 1
+            k = -side * (n // 2 - abs(j))
+            for src, dst in zip(halves(j, 0, half), halves(j, k, half)):
+                send(group + 4, src, dst, dev(k))
+
+    def gather_finish(group, n, like):
+        if n != 4:
+            take(group, like(1))
+        if n == 8:
+            take(group + 1, like(1))
+        if n > 2:
+            take(group + 4, like(n // 2 - 1))
+
+    def gather_sent(group, n, like):
+        for which in range(4 if n == 8 else n // 2):
+            sent(group + which, like(1))
+        if n > 2:
+            sent(group + 4, like(n // 2 - 1))
+
+    def g_parts(j, k):
+        return [g_all.at[pl.ds(((j - k) % nz) * cap, cap)]]
+
+    def g_halves(j, k, half):
+        return [g_all.at[pl.ds(((j - k) % nz) * cap, cap), pl.ds(half * (cols // 2), cols // 2)]]
+
+    def g_like(n):
+        return g_all.at[pl.ds(0, n * cap)]
+
+    def a_part(j, n):
+        row = ((y + j + n * (ny // 2)) % nz) * cap
+        return a_all.at[hx * c + n, pl.ds(pl.multiple_of(row, cap), cap)]
+
+    def a_parts(j, k):
+        return [a_part(j, n) for n in range(hx)]
+
+    def a_halves(j, k, half):
+        return [a_part(j, half)]
+
+    def a_like(n):
+        return a_all.at[pl.ds(hx * c, hx), pl.ds(0, n * cap)]
+
+    def own(m):
+        return jnp.where(c == 0, m, nx - 1 - m)
+
+    def f_row(m):
+        return (x + nx - own(m)) % nx
+
+    def f_parts(m):
+        return lambda j, k: [fx.at[m] if (j, k) == (0, 0) else out_ag.at[f_row(m), (z + y + j) % nz]]
+
+    def f_halves(m):
+        return lambda j, k, half: [
+            out_ag.at[f_row(m), (z + y + j) % nz, :, pl.ds(half * (heads // 2), heads // 2)]]
+
+    def f_like(n):
+        return out_ag.at[0, pl.ds(0, n)]
+
     cot_in = local(L_COT, cot_hbm, cot)
     codes_in = local(L_CODES, codes_hbm, codes)
     abs_in = local(L_ABS, abs_hbm, absm)
@@ -124,10 +198,6 @@
         pl.semaphore_signal(barrier, inc=1, device_id=dev_z(k), device_id_type=MESH)
     for k in range(1, ntp):
         pl.semaphore_signal(barrier, inc=1, device_id=dev_tp(k), device_id_type=MESH)
-
-    for i in range(nx):
-        at = pl.multiple_of((((x + i) % nx) * nz + z) * heads, heads)
-        local(L_A, attn.at[:, pl.ds(at, heads)], a_all.at[i, pl.ds(0, cap)])
 
     gate = to_column(gate_ref[...], cap)
     picked_token = to_column(sel_ref[...].astype(F32), cap)
@@ -170,66 +240,132 @@
 
     pl.semaphore_wait(barrier, (nx - 1) + (nz - 1) + (ntp - 1))
 
-    for k in range(1, nz):
-        send(S_G, g_all.at[pl.ds(0, cap)], g_all.at[pl.ds(cap * (nz - k), cap)], dev_z(k))
+    for n in range(hx):
+        off = (y + n * (ny // 2)) % nz
+        i = hx * c + n
+        dest = (z + nz - off) % nz
+        at = pl.multiple_of((((x + i) % nx) * nz + dest) * heads, heads)
+        block = attn.at[:, pl.ds(at, heads)]
+        place = a_all.at[i, pl.ds(pl.multiple_of(off * cap, cap), cap)]
+
+        @pl.when(off == 0)
+        def _():
+            local(L_A, block, place)
+
+        @pl.when(off != 0)
+        def _():
+            send(S_AZ + n, block, place, (x * nz + dest, tp))
+
+    gather_start(S_G, nz, dev_z, g_parts)
+    hh = heads // 2
+    first, second = pl.ds(0, hh), pl.ds(hh, hh)
+    send(S_W3A, w_all.at[0, first], w_all.at[3, first], dev_x(1))
+    send(S_W1A, w_all.at[0, second], w_all.at[1, second], dev_x(3))
     for k in range(1, nx):
-        send(S_W, w_all.at[0], w_all.at[nx - k], dev_x(k))
         send(S_DT, dt_all.at[0], dt_all.at[nx - k], dev_x(k))
-    for k in range(1, nz):
-        for n in range(hx):
-            i = hx * c + n
-            at = pl.multiple_of((((x + i) % nx) * nz + (z + k) % nz) * heads, heads)
-            send(S_A, attn.at[:, pl.ds(at, heads)],
-                 a_all.at[i, pl.ds(cap * (nz - k), cap)], dev_z(k))
-
-    g_rest = g_all.at[pl.ds(cap, slots - cap)]
-    w_rest = w_all.at[pl.ds(1, nx - 1)]
-    dt_rest = dt_all.at[pl.ds(1, nx - 1)]
-    a_mine = a_all.at[pl.ds(hx * c, hx), pl.ds(cap, slots - cap)]
-    a_other = a_all.at[pl.ds(hx * (1 - c), hx), pl.ds(cap, slots - cap)]
+    send(S_W3B, w_all.at[0, second], w_all.at[3, second], dev_x(1))
+    send(S_W1B, w_all.at[0, first], w_all.at[1, first], dev_x(3))
+
+    for n in range(hx):
+        off = (y + n * (ny // 2)) % nz
+
+        @pl.when(off == 0)
+        def _():
+            place = a_all.at[0, pl.ds(0, cap)]
+            pltpu.make_async_copy(place, place, lsem.at[L_A]).wait()
+
+        @pl.when(off != 0)
+        def _():
+            take(S_AZ + n, a_all.at[0, pl.ds(0, cap)])
+    gather_start(S_A, ny, dev_y, a_parts)
+    gather_forward(S_G, nz, dev_z, g_parts, g_halves, g_like)
+    half_w = w_all.at[0, first]
+    take(S_W3A, half_w)
+    send(S_W2, w_all.at[3, first], w_all.at[2, first], dev_x(1))
+    take(S_W1A, half_w)
+    send(S_W2, w_all.at[1, second], w_all.at[2, second], dev_x(3))
+    gather_forward(S_A, ny, dev_y, a_parts, a_halves, a_like)
 
     up_in.wait()
-    take(S_G, g_rest)
+    gather_finish(S_G, nz, g_like)
+    rank_part = (adapter_scale * dot(g_all[...], up[...], 1, 1)).astype(BF16)
+
+    def head_block(i):
+        part = dot(g_all[...], w_all[i], 1, 1) + dot(rank_part, dt_all[i], 1, 0)
+        for j in range(nz):
+            h_send[i, j] = part[j * cap:(j + 1) * cap].astype(BF16)
+
+    def head_pair(m):
+        send(S_HSIB + m, h_send.at[nx - 1 - own(m)], h_sib.at[m], sibling)
+
+    def head_sum(m):
+        take(S_HSIB + m, h_sib.at[m])
+        for j in range(nz):
+            hs[m, j] = (h_send[own(m), j].astype(F32) + h_sib[m, j].astype(F32)).astype(BF16)
+        for k in range(1, ny):
+            send(S_HRS + m, hs.at[m, (y + k) % ny], hr.at[m, ny - k], dev_y(k))
+
+    def head_home(m):
+        take(S_HRS + m, hr.at[m, pl.ds(1, ny - 1)])
+        total = hs[m, y].astype(F32)
+        for k in range(1, ny):
+            total = total + hr[m, k].astype(F32)
+        f_send[m] = total.astype(BF16)
+        if m == 0:
+            @pl.when(c == 0)
+            def _():
+                fx[0] = f_send[0]
+
+            @pl.when(c != 0)
+            def _():
+                send(S_FX, f_send.at[0], fx.at[0], dev_x(nx - 1))
+        else:
+            send(S_FX + m, f_send.at[m], fx.at[m], dev_x(own(m)))
+
+    def head_gather(m):
+        if m == 0:
+            @pl.when(c != 0)
+            def _():
+                take(S_FX, fx.at[0])
+        else:
+            take(S_FX + m, fx.at[m])
+        local(L_FOUT + m, fx.at[m], out_ag.at[f_row(m), shard_z])
+        gather_start(S_F0 + 5 * m, ny, dev_y, f_parts(m))
+
+    def head_forward(m):
+        gather_forward(S_F0 + 5 * m, ny, dev_y, f_parts(m), f_halves(m), f_like)
+
+    def head_finish(m):
+        gather_finish(S_F0 + 5 * m, ny, f_like)
+        pltpu.make_async_copy(fx.at[m], fx.at[m], lsem.at[L_FOUT + m]).wait()
+        send(S_FSIB + m, out_ag.at[f_row(m)], out_ag.at[f_row(m)], sibling)
+
+    shard_z = (z + y) % nz
+    take(S_DT, dt_all.at[pl.ds(1, nx - 1)])
+    head_block(0)
+    take(S_W3B, half_w)
+    head_block(3)
+    head_pair(0)
     rt[...] = adapter_scale * dot(up[...], g_all[...], 1, 1)
     send(S_RSIB, rt, rt_sib, sibling)
-    rank_part = (adapter_scale * dot(g_all[...], up[...], 1, 1)).astype(BF16)
-
-    take(S_W, w_rest)
-    take(S_DT, dt_rest)
-    for i in range(nx):
-        part = dot(g_all[...], w_all[i], 1, 1) + dot(rank_part, dt_all[i], 1, 0)
-        for j in range(nz):
-            h_send[i // hx, j, i % hx] = part[j * cap:(j + 1) * cap].astype(BF16)
-    send(S_HSIB, h_send.at[1 - c], h_sib, sibling)
-
+    take(S_W1B, half_w)
+    head_block(1)
+    head_sum(0)
+    take(S_W2, w_all.at[0])
+    head_block(2)
+    head_pair(1)
+    gather_finish(S_A, ny, a_like)
+    a_mine = a_all.at[pl.ds(hx * c, hx)]
+    send(S_ASIB, a_mine, a_mine, sibling)
     take(S_RSIB, rt_sib)
     for j in range(ny):
         rows = pl.ds(j * (rank // ny), rank // ny)
         rt_send[j] = rt[rows, :] + rt_sib[rows, :]
     for k in range(1, ny):
         send(S_RRS, rt_send.at[(y + k) % ny], rt_recv.at[ny - k], dev_y(k))
-
-    take(S_HSIB, h_sib)
-    for j in range(nz):
-        hs[j] = (h_send[c, j].astype(F32) + h_sib[j].astype(F32)).astype(BF16)
-    for k in range(1, ny):
-        send(S_HRS, hs.at[(y + k) % ny], hr.at[ny - k], dev_y(k))
-
-    take(S_RRS, rt_recv.at[pl.ds(1, ny - 1)])
-    total = rt_send[y]
-    for k in range(1, ny):
-        total = total + rt_recv[k]
-    rag_send[...] = total.astype(BF16).astype(F32)
-    rag[y] = rag_send[...]
-    for k in range(1, ny):
-        send(S_RAG, rag_send, rag.at[y], dev_y(k))
-
-    take(S_A, a_mine)
-    send(S_ASIB, a_mine, a_mine, sibling)
-    a_home = a_all.at[:, pl.ds(0, cap)]
-    pltpu.make_async_copy(a_home, a_home, lsem.at[L_A]).wait()
-    take(S_ASIB, a_other)
-
+    head_sum(1)
+
+    take(S_ASIB, a_mine)
     low = jnp.zeros((slots, rank), F32)
     low_t = jnp.zeros((rank, slots), F32)
     for i in range(nx):
@@ -252,24 +388,18 @@
     for k in range(1, nz):
         send(S_ORS, o_send.at[k], o_recv.at[nz - k], dev_z(k))
 
-    take(S_HRS, hr.at[pl.ds(1, ny - 1)])
-    total = hs[y].astype(F32)
+    take(S_RRS, rt_recv.at[pl.ds(1, ny - 1)])
+    total = rt_send[y]
     for k in range(1, ny):
-        total = total + hr[k].astype(F32)
-    f_send[...] = total.astype(BF16)
-    shard_z = (z + y) % nz
-    for n in range(hx):
-        i = hx * c + n
-        if n == 0:
-            @pl.when(c == 0)
-            def _():
-                fx[0] = f_send[0]
-
-            @pl.when(c != 0)
-            def _():
-                send(S_FX, f_send.at[0], fx.at[0], dev_x(hx))
-        else:
-            send(S_FX2 + n - 1, f_send.at[n], fx.at[n], dev_x(i))
+        total = total + rt_recv[k]
+    rag_send[...] = total.astype(BF16).astype(F32)
+    rag[y] = rag_send[...]
+    for k in range(1, ny):
+        send(S_RAG, rag_send, rag.at[y], dev_y(k))
+
+    head_home(0)
+    head_home(1)
+    head_gather(0)
 
     take(S_RAG, rag.at[pl.ds(0, ny - 1)])
     full_rt = jnp.reshape(rag[...], (rank, slots)).astype(BF16)
@@ -277,19 +407,8 @@
         d_send[i] = dot(full_rt, a_all[i], 1, 0)
     for k in range(1, nx):
         send(S_DX, d_send.at[k], d_recv.at[nx - k], dev_x(k))
-
-    for n in range(hx):
-        if n == 0:
-            @pl.when(c != 0)
-            def _():
-                take(S_FX, fx.at[0])
-        else:
-            take(S_FX2 + n - 1, fx.at[n])
-    for n in range(hx):
-        row = (x + nx - (hx * c + n)) % nx
-        local(L_FOUT, fx.at[n], out_ag.at[row, shard_z])
-        for k in range(1, ny):
-            send(S_FY, fx.at[n], out_ag.at[row, shard_z], dev_y(k))
+    head_gather(1)
+    head_forward(0)
 
     take(S_URS, u_recv.at[pl.ds(1, nz - 1)])
     total = u_send[z]
@@ -299,6 +418,7 @@
     for k in range(1, nx):
         send(S_UX, ux_send, ux_recv.at[nx - k], dev_x(k))
 
+    head_forward(1)
     take(S_ORS, o_recv.at[pl.ds(1, nz - 1)])
     block = o_home[...]
     for k in range(1, nz):
@@ -334,11 +454,8 @@
     d_new[...] = total
     d_copy = local(L_D, d_new, out_d)
 
-    take(S_FY, out_ag.at[pl.ds(0, hx), pl.ds(0, ny - 1)])
-    pltpu.make_async_copy(fx, fx, lsem.at[L_FOUT]).wait()
-    for n in range(hx):
-        row = (x + nx - (hx * c + n)) % nx
-        send(S_FSIB, out_ag.at[row], out_ag.at[row], sibling)
+    for m in range(hx):
+        head_finish(m)
 
     take(S_GG, gg_recv.at[pl.ds(1, ntp - 1)])
     total = gg_send[...]
@@ -349,30 +466,37 @@
     take(S_UAG, uag.at[pl.ds(0, nz - 1)])
     u_new[...] = jnp.reshape(uag[...], (rank, cols))
     u_copy = local(L_U, u_new, out_u)
-    take(S_FSIB, out_ag.at[pl.ds(0, hx)])
+    for m in range(hx):
+        take(S_FSIB + m, out_ag.at[0])
 
     out_copy.wait()
     d_copy.wait()
     u_copy.wait()
-    sent(S_G, g_rest)
-    sent(S_W, w_rest)
-    sent(S_DT, dt_rest)
-    sent(S_A, a_mine)
+    for n in range(hx):
+        @pl.when((y + n * (ny // 2)) % nz != 0)
+        def _():
+            sent(S_AZ + n, a_all.at[0, pl.ds(0, cap)])
+    gather_sent(S_G, nz, g_like)
+    gather_sent(S_A, ny, a_like)
+    for m in range(hx):
+        gather_sent(S_F0 + 5 * m, ny, f_like)
+    for group in (S_W1A, S_W1B, S_W3A, S_W3B):
+        sent(group, half_w)
+    sent(S_W2, w_all.at[0])
+    sent(S_DT, dt_all.at[pl.ds(1, nx - 1)])
     sent(S_ASIB, a_mine)
     sent(S_RSIB, rt)
     sent(S_RRS, rt_recv.at[pl.ds(1, ny - 1)])
     sent(S_RAG, rag.at[pl.ds(0, ny - 1)])
-    sent(S_HSIB, h_sib)
-    sent(S_HRS, hr.at[pl.ds(1, ny - 1)])
-    for n in range(hx):
-        if n == 0:
-            @pl.when(c != 0)
-            def _():
-                sent(S_FX, fx.at[0])
-        else:
-            sent(S_FX2 + n - 1, fx.at[n])
-    sent(S_FY, out_ag.at[pl.ds(0, hx), pl.ds(0, ny - 1)])
-    sent(S_FSIB, out_ag.at[pl.ds(0, hx)])
+    for m in range(hx):
+        sent(S_HSIB + m, h_sib.at[m])
+        sent(S_HRS + m, hr.at[m, pl.ds(1, ny - 1)])
+        sent(S_FSIB + m, out_ag.at[0])
+
+    @pl.when(c != 0)
+    def _():
+        sent(S_FX, fx.at[0])
+    sent(S_FX + 1, fx.at[1])
     sent(S_URS, u_recv.at[pl.ds(1, nz - 1)])
     sent(S_UAG, uag.at[pl.ds(0, nz - 1)])
     sent(S_ORS, o_recv.at[pl.ds(1, nz - 1)])
@@ -414,8 +538,8 @@
             bf16(nx, slots, heads), bf16(nx, heads, cols), bf16(nx, rank, heads), bf16(slots, cols),
             f32(rank, slots), f32(rank, slots), f32(ny, rank // ny, slots), f32(ny, rank // ny, slots),
             f32(rank // ny, slots), f32(ny, rank // ny, slots),
-            bf16(NC, nz, hx, cap, heads), bf16(nz, hx, cap, heads), bf16(nz, hx, cap, heads),
-            bf16(ny, hx, cap, heads), bf16(hx, cap, heads), bf16(hx, cap, heads),
+            bf16(nx, nz, cap, heads), bf16(hx, nz, cap, heads), bf16(hx, nz, cap, heads),
+            bf16(hx, ny, cap, heads), bf16(hx, cap, heads), bf16(hx, cap, heads),
             f32(nz, rank // nz, cols), f32(nz, rank // nz, cols), f32(rank // nz, cols),
             f32(nx, rank // nz, cols), f32(nz, rank // nz, cols),
             bf16(nz, cap, cols), bf16(nz, cap, cols), f32(cap, cols), bf16(tokens, cols),

time: 69.3 us -> 66.6 us (0.961)
  Pallas kernels: 61.5 us -> 59.2 us
    pallas_call x1, Pallas kernels: 61.5 us -> 59.2 us  [body(): pl.pallas_call(functools.partial(kernel, nx, nz, ny), out_shape=(jax.Shap...]
where the time goes in v2:
time: 66.6 us; the launch traced here: 66.3 us
  Pallas kernels  59.2 us (89%)
  local copies, waits for them, and re-layouts  5.81 us (9%)
  between operations  1.29 us (2%)
    pallas_call x1, Pallas kernels, body(): pl.pallas_call(functools.partial(kernel, nx, nz, ny), out_shape=(jax.Shap...  59.2 us
    unnamed x11, local copies, waits for them, and re-layouts  5.81 us

profile of v2, /device:TPU:1, one launch (start us, length us, event | category | flops | bytes accessed | tf_op | source)
XLA Modules:
  0.0 66.3 jit_solution(5385343015405863543)
XLA Ops:
  1.3 59.2 %block_step.1 = (bf16[192,512]{1,0:T(8,128)(2,1)}, bf16[4,8,48,256]{3,2,1,0:T(8,128)(2,1)}, f32[64,256]{1,0:T(8,128)}, f32[64,512]{1,0:T(8,128)}, f32[1,48]{1,0:T(1,128)}) custom-call(bf16[192,512]{1,0:T(8,128)(2,1)} %res_hbm.1, bf16[48,8192]{1,0:T(8,128)(2,1)} %attn.1, s32[256,512]{1,0:T(8,128)} %codes_hbm.1, f32[8,256]{1,0:T(8,128)} %bitcast.12, ...), custom_call_target="tpu_custom_call" | custom-call | tf_op jit(solution)/shard_map/block_step/pallas_call | solution.py:524
  60.5 1.6 %copy.21 = bf16[192,512]{1,0:T(8,128)(2,1)} copy(bf16[192,512]{1,0:T(8,128)(2,1)} %get-tuple-element.20) | data formatting | bytes 393216
  62.1 0.0 copy-start.1
  62.2 2.1 %copy.22 = bf16[1536,256]{1,0:T(8,128)(2,1)} copy(bf16[1536,256]{1,0:T(8,128)(2,1)} %bitcast.9) | data formatting | bytes 1572864
  64.2 0.0 copy-done.1
  64.2 0.0 copy-start
  64.3 0.6 copy.23
  64.9 0.3 copy-done
  65.2 0.0 copy-start.2
  65.2 0.7 copy.24
  65.8 0.0 copy-done.2
  65.8 0.5 copy.25
Async XLA Ops:
  62.1 2.1 %copy-start.1 = (f32[64,256]{1,0:T(8,128)S(1)}, f32[64,256]{1,0:T(8,128)}, u32[]{:S(2)}) copy-start(f32[64,256]{1,0:T(8,128)} %get-tuple-element.12) | copy-start | bytes 196612
  64.2 0.9 %copy-start = (f32[64,512]{1,0:T(8,128)S(1)}, f32[64,512]{1,0:T(8,128)}, u32[]{:S(2)}) copy-start(f32[64,512]{1,0:T(8,128)} %get-tuple-element.23) | copy-start | bytes 393220
  65.2 0.7 copy-start.2

commit v3 on v2

--- a/solution.py
+++ b/solution.py
@@ -31,10 +31,10 @@
 
 NX, NZ, NY, NC = 4, 8, 8, 2
 
-(S_G, S_A, S_F0, S_F1, S_AZ, S_W1A, S_W1B, S_W3A, S_W3B, S_W2, S_DT, S_ASIB, S_RSIB, S_RRS, S_RAG,
- S_HSIB, S_HRS, S_FX, S_FSIB, S_URS, S_UX, S_UAG, S_ORS, S_DX, S_GG, N_SEM) = (
-    0, 5, 10, 15, 20, *range(22, 32), 32, 34, 36, 38, *range(40, 47))
-(L_COT, L_CODES, L_ABS, L_DOWN, L_UP, L_RES, L_A, L_OUT, L_D, L_U, L_FOUT, N_LOC) = (*range(11), 12)
+(S_G, S_A, S_F, S_AZ, S_W1A, S_W1B, S_W3A, S_W3B, S_W2, S_DT, S_ASIB, S_RSIB, S_RRS, S_RAG,
+ S_HSIB, S_HRS, S_FSIB, S_URS, S_UX, S_UAG, S_ORS, S_DX, S_GG, N_SEM) = (
+    0, 1, 2, 4, *range(6, 16), 16, 18, 20, *range(22, 29))
+(L_COT, L_CODES, L_ABS, L_DOWN, L_UP, L_RES, L_A, L_OUT, L_D, L_U, L_FOUT, N_LOC) = range(12)
 
 
 def dot(a, b, ca, cb):
@@ -62,7 +62,7 @@
            res, codes, absm, up, cot, scales,
            a_all, w_all, dt_all, g_all,
            rt, rt_sib, rt_send, rt_recv, rag_send, rag,
-           h_send, h_sib, hs, hr, f_send, fx,
+           h_send, h_sib, hs, hr, f_send,
            u_send, u_recv, ux_send, ux_recv, uag,
            o_send, o_recv, o_home, new_res,
            d_send, d_recv, d_new, u_new, gg_send, gg_recv,
@@ -111,46 +111,13 @@
         copy.start()
         return copy
 
-    def gather_start(group, n, dev, parts):
-        for k in sorted({1, n - 1} | ({2, n - 2} if n == 8 else set())):
-            which = {n - 1: 0, 1: 1, n - 2: 2, 2: 3}[n - k] if n > 2 else 0
+    def gather(group, n, dev, parts):
+        for k in (range(1, n) if n < 8 else (1, 7, 2, 6, 3, 5, 4)):
             for src, dst in zip(parts(0, 0), parts(0, k)):
-                send(group + which, src, dst, dev(k))
-
-    def gather_forward(group, n, dev, parts, halves, like):
-        if n == 2:
-            return
-        far = n // 2 - 2
-        for side, which in ((-1, 2 if far else 0), (1, 3 if far else 1)):
-            j = side * (far if far else 1)
-            take(group + which, like(1))
-            if far:
-                for src, dst in zip(parts(j, 0), parts(j, -side)):
-                    send(group + 4, src, dst, dev(-side))
-            half = 0 if side < 0 else 1
-            k = -side * (n // 2 - abs(j))
-            for src, dst in zip(halves(j, 0, half), halves(j, k, half)):
-                send(group + 4, src, dst, dev(k))
-
-    def gather_finish(group, n, like):
-        if n != 4:
-            take(group, like(1))
-        if n == 8:
-            take(group + 1, like(1))
-        if n > 2:
-            take(group + 4, like(n // 2 - 1))
-
-    def gather_sent(group, n, like):
-        for which in range(4 if n == 8 else n // 2):
-            sent(group + which, like(1))
-        if n > 2:
-            sent(group + 4, like(n // 2 - 1))
+                send(group, src, dst, dev(k))
 
     def g_parts(j, k):
         return [g_all.at[pl.ds(((j - k) % nz) * cap, cap)]]
-
-    def g_halves(j, k, half):
-        return [g_all.at[pl.ds(((j - k) % nz) * cap, cap), pl.ds(half * (cols // 2), cols // 2)]]
 
     def g_like(n):
         return g_all.at[pl.ds(0, n * cap)]
@@ -162,27 +129,17 @@
     def a_parts(j, k):
         return [a_part(j, n) for n in range(hx)]
 
-    def a_halves(j, k, half):
-        return [a_part(j, half)]
-
     def a_like(n):
         return a_all.at[pl.ds(hx * c, hx), pl.ds(0, n * cap)]
 
     def own(m):
         return jnp.where(c == 0, m, nx - 1 - m)
 
+    def f_like(n):
+        return out_ag.at[0, pl.ds(0, n)]
+
     def f_row(m):
         return (x + nx - own(m)) % nx
-
-    def f_parts(m):
-        return lambda j, k: [fx.at[m] if (j, k) == (0, 0) else out_ag.at[f_row(m), (z + y + j) % nz]]
-
-    def f_halves(m):
-        return lambda j, k, half: [
-            out_ag.at[f_row(m), (z + y + j) % nz, :, pl.ds(half * (heads // 2), heads // 2)]]
-
-    def f_like(n):
-        return out_ag.at[0, pl.ds(0, n)]
 
     cot_in = local(L_COT, cot_hbm, cot)
     codes_in = local(L_CODES, codes_hbm, codes)
@@ -256,7 +213,7 @@
         def _():
             send(S_AZ + n, block, place, (x * nz + dest, tp))
 
-    gather_start(S_G, nz, dev_z, g_parts)
+    gather(S_G, nz, dev_z, g_parts)
     hh = heads // 2
     first, second = pl.ds(0, hh), pl.ds(hh, hh)
     send(S_W3A, w_all.at[0, first], w_all.at[3, first], dev_x(1))
@@ -277,17 +234,15 @@
         @pl.when(off != 0)
         def _():
             take(S_AZ + n, a_all.at[0, pl.ds(0, cap)])
-    gather_start(S_A, ny, dev_y, a_parts)
-    gather_forward(S_G, nz, dev_z, g_parts, g_halves, g_like)
+    gather(S_A, ny, dev_y, a_parts)
     half_w = w_all.at[0, first]
     take(S_W3A, half_w)
     send(S_W2, w_all.at[3, first], w_all.at[2, first], dev_x(1))
     take(S_W1A, half_w)
     send(S_W2, w_all.at[1, second], w_all.at[2, second], dev_x(3))
-    gather_forward(S_A, ny, dev_y, a_parts, a_halves, a_like)
 
     up_in.wait()
-    gather_finish(S_G, nz, g_like)
+    take(S_G, g_like(nz - 1))
     rank_part = (adapter_scale * dot(g_all[...], up[...], 1, 1)).astype(BF16)
 
     def head_block(i):
@@ -311,33 +266,33 @@
         for k in range(1, ny):
             total = total + hr[m, k].astype(F32)
         f_send[m] = total.astype(BF16)
+        near = ((x + own(m)) % nx) * nz + z
+        place = out_ag.at[x, shard_z]
+        for k in (range(1, ny) if ny < 8 else (4, 3, 5, 2, 6, 1, 7)):
+            send(S_F + m, f_send.at[m], place, (near, ((y + k) % ny) * NC + c))
         if m == 0:
             @pl.when(c == 0)
             def _():
-                fx[0] = f_send[0]
+                local(L_FOUT, f_send.at[0], place)
 
             @pl.when(c != 0)
             def _():
-                send(S_FX, f_send.at[0], fx.at[0], dev_x(nx - 1))
+                send(S_F, f_send.at[0], place, (near, tp))
         else:
-            send(S_FX + m, f_send.at[m], fx.at[m], dev_x(own(m)))
-
-    def head_gather(m):
+            send(S_F + m, f_send.at[m], place, (near, tp))
+
+    def head_finish(m):
         if m == 0:
+            @pl.when(c == 0)
+            def _():
+                take(S_F, f_like(ny - 1))
+                pltpu.make_async_copy(f_send.at[0], f_send.at[0], lsem.at[L_FOUT]).wait()
+
             @pl.when(c != 0)
             def _():
-                take(S_FX, fx.at[0])
+                take(S_F, f_like(ny))
         else:
-            take(S_FX + m, fx.at[m])
-        local(L_FOUT + m, fx.at[m], out_ag.at[f_row(m), shard_z])
-        gather_start(S_F0 + 5 * m, ny, dev_y, f_parts(m))
-
-    def head_forward(m):
-        gather_forward(S_F0 + 5 * m, ny, dev_y, f_parts(m), f_halves(m), f_like)
-
-    def head_finish(m):
-        gather_finish(S_F0 + 5 * m, ny, f_like)
-        pltpu.make_async_copy(fx.at[m], fx.at[m], lsem.at[L_FOUT + m]).wait()
+            take(S_F + m, f_like(ny))
         send(S_FSIB + m, out_ag.at[f_row(m)], out_ag.at[f_row(m)], sibling)
 
     shard_z = (z + y) % nz
@@ -354,7 +309,7 @@
     take(S_W2, w_all.at[0])
     head_block(2)
     head_pair(1)
-    gather_finish(S_A, ny, a_like)
+    take(S_A, a_like(ny - 1))
     a_mine = a_all.at[pl.ds(hx * c, hx)]
     send(S_ASIB, a_mine, a_mine, sibling)
     take(S_RSIB, rt_sib)
@@ -399,7 +354,6 @@
 
     head_home(0)
     head_home(1)
-    head_gather(0)
 
     take(S_RAG, rag.at[pl.ds(0, ny - 1)])
     full_rt = jnp.reshape(rag[...], (rank, slots)).astype(BF16)
@@ -407,8 +361,6 @@
         d_send[i] = dot(full_rt, a_all[i], 1, 0)
     for k in range(1, nx):
         send(S_DX, d_send.at[k], d_recv.at[nx - k], dev_x(k))
-    head_gather(1)
-    head_forward(0)
 
     take(S_URS, u_recv.at[pl.ds(1, nz - 1)])
     total = u_send[z]
@@ -418,7 +370,8 @@
     for k in range(1, nx):
         send(S_UX, ux_send, ux_recv.at[nx - k], dev_x(k))
 
-    head_forward(1)
+    head_finish(0)
+
     take(S_ORS, o_recv.at[pl.ds(1, nz - 1)])
     block = o_home[...]
     for k in range(1, nz):
@@ -454,8 +407,7 @@
     d_new[...] = total
     d_copy = local(L_D, d_new, out_d)
 
-    for m in range(hx):
-        head_finish(m)
+    head_finish(1)
 
     take(S_GG, gg_recv.at[pl.ds(1, ntp - 1)])
     total = gg_send[...]
@@ -476,10 +428,17 @@
         @pl.when((y + n * (ny // 2)) % nz != 0)
         def _():
             sent(S_AZ + n, a_all.at[0, pl.ds(0, cap)])
-    gather_sent(S_G, nz, g_like)
-    gather_sent(S_A, ny, a_like)
-    for m in range(hx):
-        gather_sent(S_F0 + 5 * m, ny, f_like)
+    sent(S_G, g_like(nz - 1))
+    sent(S_A, a_like(ny - 1))
+
+    @pl.when(c == 0)
+    def _():
+        sent(S_F, f_like(ny - 1))
+
+    @pl.when(c != 0)
+    def _():
+        sent(S_F, f_like(ny))
+    sent(S_F + 1, f_like(ny))
     for group in (S_W1A, S_W1B, S_W3A, S_W3B):
         sent(group, half_w)
     sent(S_W2, w_all.at[0])
@@ -493,15 +452,26 @@
         sent(S_HRS + m, hr.at[m, pl.ds(1, ny - 1)])
         sent(S_FSIB + m, out_ag.at[0])
 
-    @pl.when(c != 0)
-    def _():
-        sent(S_FX, fx.at[0])
-    sent(S_FX + 1, fx.at[1])
     sent(S_URS, u_recv.at[pl.ds(1, nz - 1)])
     sent(S_UAG, uag.at[pl.ds(0, nz - 1)])
     sent(S_ORS, o_recv.at[pl.ds(1, nz - 1)])
     sent(S_DX, d_recv.at[pl.ds(1, nx - 1)])
     sent(S_GG, gg_recv.at[pl.ds(1, ntp - 1)])
+
+
+def hand_over(*refs):
+    n = (len(refs) - 1) // 2
+    sems = refs[-1]
+    copies = []
+    for src, dst in zip(refs[:n], refs[n:2 * n]):
+        pieces = src.shape[0] if len(src.shape) == 4 else 1
+        for piece in range(pieces):
+            at = pl.ds(piece, 1) if pieces > 1 else slice(None)
+            copies.append(pltpu.make_async_copy(src.at[at], dst.at[at], sems.at[len(copies)]))
+    for copy in copies:
+        copy.start()
+    for copy in copies:
+        copy.wait()
 
 
 def body(residual, attention, codes, absmax, down, up, gate, selected, counts, cotangent,
@@ -539,7 +509,7 @@
             f32(rank, slots), f32(rank, slots), f32(ny, rank // ny, slots), f32(ny, rank // ny, slots),
             f32(rank // ny, slots), f32(ny, rank // ny, slots),
             bf16(nx, nz, cap, heads), bf16(hx, nz, cap, heads), bf16(hx, nz, cap, heads),
-            bf16(hx, ny, cap, heads), bf16(hx, cap, heads), bf16(hx, cap, heads),
+            bf16(hx, ny, cap, heads), bf16(hx, cap, heads),
             f32(nz, rank // nz, cols), f32(nz, rank // nz, cols), f32(rank // nz, cols),
             f32(nx, rank // nz, cols), f32(nz, rank // nz, cols),
             bf16(nz, cap, cols), bf16(nz, cap, cols), f32(cap, cols), bf16(tokens, cols),
@@ -553,7 +523,14 @@
         name="block_step",
     )(residual, attention, codes, absmax.T, down.T, up, gate.reshape(1, cap), selected.reshape(1, cap),
       counts.reshape(1, 1), cotangent)
-    new_res, head_grad, d_grad, u_grad, g_grad = outs
+    new_res, head_grad, d_grad, u_grad, g_grad = pl.pallas_call(
+        hand_over,
+        out_shape=[jax.ShapeDtypeStruct(out.shape, out.dtype) for out in outs],
+        in_specs=[anywhere] * 5,
+        out_specs=[anywhere] * 5,
+        scratch_shapes=[pltpu.SemaphoreType.DMA((nx + 4,))],
+        name="hand_over",
+    )(*outs)
     return new_res, head_grad.reshape(nx * nz * cap, heads), d_grad.T, u_grad, g_grad.reshape(cap)
 
 

time: 66.6 us -> 103 us (1.55)
  Pallas kernels: 59.2 us -> 101 us
  local copies, waits for them, and re-layouts: 5.81 us -> 0 us
    pallas_call x0 -> x1, Pallas kernels: none -> 36.9 us  [body(): pl.pallas_call(hand_over, out_shape=[jax.ShapeDtypeStruct(out.shape, out....]
    unnamed x11 -> x0, local copies, waits for them, and re-layouts: 5.81 us -> none
    pallas_call x1, Pallas kernels: 59.2 us -> 64.5 us  [body(): pl.pallas_call(functools.partial(kernel, nx, nz, ny), out_shape=(jax.Shap...]
where the time goes in v3:
time: 103 us
  Pallas kernels  101 us (98%)
  between operations  1.29 us (1%)
    pallas_call x1, Pallas kernels, body(): pl.pallas_call(functools.partial(kernel, nx, nz, ny), out_shape=(jax.Shap...  64.5 us
    pallas_call x1, Pallas kernels, body(): pl.pallas_call(hand_over, out_shape=[jax.ShapeDtypeStruct(out.shape, out....  36.9 us

profile of v3, /device:TPU:1, one launch (start us, length us, event | category | flops | bytes accessed | tf_op | source)
XLA Modules:
  0.0 102.7 jit_solution(13754271341968422502)
XLA Ops:
  1.3 64.5 %block_step.1 = (bf16[192,512]{1,0:T(8,128)(2,1)}, bf16[4,8,48,256]{3,2,1,0:T(8,128)(2,1)}, f32[64,256]{1,0:T(8,128)}, f32[64,512]{1,0:T(8,128)}, f32[1,48]{1,0:T(1,128)}) custom-call(bf16[192,512]{1,0:T(8,128)(2,1)} %res_hbm.1, bf16[48,8192]{1,0:T(8,128)(2,1)} %attn.1, s32[256,512]{1,0:T(8,128)} %codes_hbm.1, f32[8,256]{1,0:T(8,128)} %bitcast.10, ...), custom_call_target="tpu_custom_call" | custom-call | tf_op jit(solution)/shard_map/block_step/pallas_call | solution.py:494
  65.8 36.9 %hand_over.1 = (bf16[192,512]{1,0:T(8,128)(2,1)}, bf16[4,8,48,256]{3,2,1,0:T(8,128)(2,1)}, f32[64,256]{1,0:T(8,128)}, f32[64,512]{1,0:T(8,128)}, f32[1,48]{1,0:T(1,128)}) custom-call(bf16[192,512]{1,0:T(8,128)(2,1)} %get-tuple-element.15.refs_0_, bf16[4,8,48,256]{3,2,1,0:T(8,128)(2,1)} %get-tuple-element.16.refs_1_, f32[64,256]{1,0:T(8,128)} %get-tuple-element.17.refs_2_, ...), custom_call_target="tpu_custom_call" | custom-call | tf_op jit(solution)/shard_map/hand_over/pallas_call | solution.py:526

commit v4 on v3

--- a/solution.py
+++ b/solution.py
@@ -34,7 +34,7 @@
 (S_G, S_A, S_F, S_AZ, S_W1A, S_W1B, S_W3A, S_W3B, S_W2, S_DT, S_ASIB, S_RSIB, S_RRS, S_RAG,
  S_HSIB, S_HRS, S_FSIB, S_URS, S_UX, S_UAG, S_ORS, S_DX, S_GG, N_SEM) = (
     0, 1, 2, 4, *range(6, 16), 16, 18, 20, *range(22, 29))
-(L_COT, L_CODES, L_ABS, L_DOWN, L_UP, L_RES, L_A, L_OUT, L_D, L_U, L_FOUT, N_LOC) = range(12)
+(L_COT, L_CODES, L_ABS, L_DOWN, L_UP, L_RES, L_A, L_OUT, L_D, L_U, L_FOUT, L_AG, N_LOC) = (*range(12), 15)
 
 
 def dot(a, b, ca, cb):
@@ -62,7 +62,7 @@
            res, codes, absm, up, cot, scales,
            a_all, w_all, dt_all, g_all,
            rt, rt_sib, rt_send, rt_recv, rag_send, rag,
-           h_send, h_sib, hs, hr, f_send,
+           h_send, h_sib, hs, hr, f_send, og,
            u_send, u_recv, ux_send, ux_recv, uag,
            o_send, o_recv, o_home, new_res,
            d_send, d_recv, d_new, u_new, gg_send, gg_recv,
@@ -136,7 +136,7 @@
         return jnp.where(c == 0, m, nx - 1 - m)
 
     def f_like(n):
-        return out_ag.at[0, pl.ds(0, n)]
+        return og.at[0, pl.ds(0, n)]
 
     def f_row(m):
         return (x + nx - own(m)) % nx
@@ -267,7 +267,7 @@
             total = total + hr[m, k].astype(F32)
         f_send[m] = total.astype(BF16)
         near = ((x + own(m)) % nx) * nz + z
-        place = out_ag.at[x, shard_z]
+        place = og.at[x, shard_z]
         for k in (range(1, ny) if ny < 8 else (4, 3, 5, 2, 6, 1, 7)):
             send(S_F + m, f_send.at[m], place, (near, ((y + k) % ny) * NC + c))
         if m == 0:
@@ -293,7 +293,8 @@
                 take(S_F, f_like(ny))
         else:
             take(S_F + m, f_like(ny))
-        send(S_FSIB + m, out_ag.at[f_row(m)], out_ag.at[f_row(m)], sibling)
+        send(S_FSIB + m, og.at[f_row(m)], og.at[f_row(m)], sibling)
+        local(L_AG + m, og.at[f_row(m)], out_ag.at[f_row(m)])
 
     shard_z = (z + y) % nz
     take(S_DT, dt_all.at[pl.ds(1, nx - 1)])
@@ -419,8 +420,12 @@
     u_new[...] = jnp.reshape(uag[...], (rank, cols))
     u_copy = local(L_U, u_new, out_u)
     for m in range(hx):
-        take(S_FSIB + m, out_ag.at[0])
-
+        take(S_FSIB + m, og.at[0])
+        row = (x + nx - (nx - 1 - own(m))) % nx
+        local(L_AG + hx + m, og.at[row], out_ag.at[row])
+
+    for m in range(2 * hx):
+        pltpu.make_async_copy(og.at[0], og.at[0], lsem.at[L_AG + m]).wait()
     out_copy.wait()
     d_copy.wait()
     u_copy.wait()
@@ -450,7 +455,7 @@
     for m in range(hx):
         sent(S_HSIB + m, h_sib.at[m])
         sent(S_HRS + m, hr.at[m, pl.ds(1, ny - 1)])
-        sent(S_FSIB + m, out_ag.at[0])
+        sent(S_FSIB + m, og.at[0])
 
     sent(S_URS, u_recv.at[pl.ds(1, nz - 1)])
     sent(S_UAG, uag.at[pl.ds(0, nz - 1)])
@@ -460,17 +465,21 @@
 
 
 def hand_over(*refs):
-    n = (len(refs) - 1) // 2
-    sems = refs[-1]
-    copies = []
-    for src, dst in zip(refs[:n], refs[n:2 * n]):
+    n = len(refs) // 3
+    srcs, dsts, held, into, out_of = refs[:n], refs[n:2 * n], refs[2 * n:3 * n], refs[-2], refs[-1]
+    ins, outs = [], []
+    for src, dst, mid in zip(srcs, dsts, held):
         pieces = src.shape[0] if len(src.shape) == 4 else 1
         for piece in range(pieces):
             at = pl.ds(piece, 1) if pieces > 1 else slice(None)
-            copies.append(pltpu.make_async_copy(src.at[at], dst.at[at], sems.at[len(copies)]))
-    for copy in copies:
+            ins.append(pltpu.make_async_copy(src.at[at], mid.at[at], into.at[len(ins)]))
+            outs.append(pltpu.make_async_copy(mid.at[at], dst.at[at], out_of.at[len(outs)]))
+    for copy in ins:
         copy.start()
-    for copy in copies:
+    for copy, onward in zip(ins, outs):
+        copy.wait()
+        onward.start()
+    for copy in outs:
         copy.wait()
 
 
@@ -509,7 +518,7 @@
             f32(rank, slots), f32(rank, slots), f32(ny, rank // ny, slots), f32(ny, rank // ny, slots),
             f32(rank // ny, slots), f32(ny, rank // ny, slots),
             bf16(nx, nz, cap, heads), bf16(hx, nz, cap, heads), bf16(hx, nz, cap, heads),
-            bf16(hx, ny, cap, heads), bf16(hx, cap, heads),
+            bf16(hx, ny, cap, heads), bf16(hx, cap, heads), bf16(nx, nz, cap, heads),
             f32(nz, rank // nz, cols), f32(nz, rank // nz, cols), f32(rank // nz, cols),
             f32(nx, rank // nz, cols), f32(nz, rank // nz, cols),
             bf16(nz, cap, cols), bf16(nz, cap, cols), f32(cap, cols), bf16(tokens, cols),
@@ -528,7 +537,8 @@
         out_shape=[jax.ShapeDtypeStruct(out.shape, out.dtype) for out in outs],
         in_specs=[anywhere] * 5,
         out_specs=[anywhere] * 5,
-        scratch_shapes=[pltpu.SemaphoreType.DMA((nx + 4,))],
+        scratch_shapes=[pltpu.VMEM(out.shape, out.dtype) for out in outs]
+        + [pltpu.SemaphoreType.DMA((nx + 4,))] * 2,
         name="hand_over",
     )(*outs)
     return new_res, head_grad.reshape(nx * nz * cap, heads), d_grad.T, u_grad, g_grad.reshape(cap)

time: 103 us -> 68.4 us (0.66)
  Pallas kernels: 101 us -> 66.8 us
    pallas_call x1, Pallas kernels: 36.9 us -> 2.17 us  [body(): pl.pallas_call(hand_over, out_shape=[jax.ShapeDtypeStruct(out.shape, out....]
where the time goes in v4:
time: 68.4 us; the launch traced here: 68.1 us
  Pallas kernels  66.8 us (98%)
  between operations  1.29 us (2%)
    pallas_call x1, Pallas kernels, body(): pl.pallas_call(functools.partial(kernel, nx, nz, ny), out_shape=(jax.Shap...  64.7 us
    pallas_call x1, Pallas kernels, body(): pl.pallas_call(hand_over, out_shape=[jax.ShapeDtypeStruct(out.shape, out....  2.17 us

profile of v4, /device:TPU:1, one launch (start us, length us, event | category | flops | bytes accessed | tf_op | source)
XLA Modules:
  0.0 68.1 jit_solution(9755147316066519187)
XLA Ops:
  1.3 64.7 %block_step.1 = (bf16[192,512]{1,0:T(8,128)(2,1)}, bf16[4,8,48,256]{3,2,1,0:T(8,128)(2,1)}, f32[64,256]{1,0:T(8,128)}, f32[64,512]{1,0:T(8,128)}, f32[1,48]{1,0:T(1,128)}) custom-call(bf16[192,512]{1,0:T(8,128)(2,1)} %res_hbm.1, bf16[48,8192]{1,0:T(8,128)(2,1)} %attn.1, s32[256,512]{1,0:T(8,128)} %codes_hbm.1, f32[8,256]{1,0:T(8,128)} %bitcast.10, ...), custom_call_target="tpu_custom_call" | custom-call | tf_op jit(solution)/shard_map/block_step/pallas_call | solution.py:503
  66.0 2.2 %hand_over.1 = (bf16[192,512]{1,0:T(8,128)(2,1)}, bf16[4,8,48,256]{3,2,1,0:T(8,128)(2,1)}, f32[64,256]{1,0:T(8,128)}, f32[64,512]{1,0:T(8,128)}, f32[1,48]{1,0:T(1,128)}) custom-call(bf16[192,512]{1,0:T(8,128)(2,1)} %get-tuple-element.15.refs_0_, bf16[4,8,48,256]{3,2,1,0:T(8,128)(2,1)} %get-tuple-element.16.refs_1_, f32[64,256]{1,0:T(8,128)} %get-tuple-element.17.refs_2_, ...), custom_call_target="tpu_custom_call" | custom-call | tf_op jit(solution)/shard_map/hand_over/pallas_call | solution.py:535

commit v5 on v2

--- a/solution.py
+++ b/solution.py
@@ -34,7 +34,8 @@
 (S_G, S_A, S_F0, S_F1, S_AZ, S_W1A, S_W1B, S_W3A, S_W3B, S_W2, S_DT, S_ASIB, S_RSIB, S_RRS, S_RAG,
  S_HSIB, S_HRS, S_FX, S_FSIB, S_URS, S_UX, S_UAG, S_ORS, S_DX, S_GG, N_SEM) = (
     0, 5, 10, 15, 20, *range(22, 32), 32, 34, 36, 38, *range(40, 47))
-(L_COT, L_CODES, L_ABS, L_DOWN, L_UP, L_RES, L_A, L_OUT, L_D, L_U, L_FOUT, N_LOC) = (*range(11), 12)
+DIRECT = (S_A,)
+(L_COT, L_CODES, L_ABS, L_DOWN, L_UP, L_RES, L_A, L_OUT, L_D, L_U, L_FOUT, L_AG, N_LOC) = (*range(11), 12, 16)
 
 
 def dot(a, b, ca, cb):
@@ -62,7 +63,7 @@
            res, codes, absm, up, cot, scales,
            a_all, w_all, dt_all, g_all,
            rt, rt_sib, rt_send, rt_recv, rag_send, rag,
-           h_send, h_sib, hs, hr, f_send, fx,
+           h_send, h_sib, hs, hr, f_send, fx, og,
            u_send, u_recv, ux_send, ux_recv, uag,
            o_send, o_recv, o_home, new_res,
            d_send, d_recv, d_new, u_new, gg_send, gg_recv,
@@ -112,13 +113,18 @@
         return copy
 
     def gather_start(group, n, dev, parts):
+        if n == 8 and group in DIRECT:
+            for k in (1, 7, 2, 6, 3, 5, 4):
+                for src, dst in zip(parts(0, 0), parts(0, k)):
+                    send(group, src, dst, dev(k))
+            return
         for k in sorted({1, n - 1} | ({2, n - 2} if n == 8 else set())):
             which = {n - 1: 0, 1: 1, n - 2: 2, 2: 3}[n - k] if n > 2 else 0
             for src, dst in zip(parts(0, 0), parts(0, k)):
                 send(group + which, src, dst, dev(k))
 
     def gather_forward(group, n, dev, parts, halves, like):
-        if n == 2:
+        if n == 2 or (n == 8 and group in DIRECT):
             return
         far = n // 2 - 2
         for side, which in ((-1, 2 if far else 0), (1, 3 if far else 1)):
@@ -133,6 +139,9 @@
                 send(group + 4, src, dst, dev(k))
 
     def gather_finish(group, n, like):
+        if n == 8 and group in DIRECT:
+            take(group, like(n - 1))
+            return
         if n != 4:
             take(group, like(1))
         if n == 8:
@@ -141,6 +150,9 @@
             take(group + 4, like(n // 2 - 1))
 
     def gather_sent(group, n, like):
+        if n == 8 and group in DIRECT:
+            sent(group, like(n - 1))
+            return
         for which in range(4 if n == 8 else n // 2):
             sent(group + which, like(1))
         if n > 2:
@@ -175,14 +187,14 @@
         return (x + nx - own(m)) % nx
 
     def f_parts(m):
-        return lambda j, k: [fx.at[m] if (j, k) == (0, 0) else out_ag.at[f_row(m), (z + y + j) % nz]]
+        return lambda j, k: [fx.at[m] if (j, k) == (0, 0) else og.at[f_row(m), (z + y + j) % nz]]
 
     def f_halves(m):
         return lambda j, k, half: [
-            out_ag.at[f_row(m), (z + y + j) % nz, :, pl.ds(half * (heads // 2), heads // 2)]]
+            og.at[f_row(m), (z + y + j) % nz, :, pl.ds(half * (heads // 2), heads // 2)]]
 
     def f_like(n):
-        return out_ag.at[0, pl.ds(0, n)]
+        return og.at[0, pl.ds(0, n)]
 
     cot_in = local(L_COT, cot_hbm, cot)
     codes_in = local(L_CODES, codes_hbm, codes)
@@ -329,7 +341,7 @@
                 take(S_FX, fx.at[0])
         else:
             take(S_FX + m, fx.at[m])
-        local(L_FOUT + m, fx.at[m], out_ag.at[f_row(m), shard_z])
+        local(L_FOUT + m, fx.at[m], og.at[f_row(m), shard_z])
         gather_start(S_F0 + 5 * m, ny, dev_y, f_parts(m))
 
     def head_forward(m):
@@ -338,7 +350,8 @@
     def head_finish(m):
         gather_finish(S_F0 + 5 * m, ny, f_like)
         pltpu.make_async_copy(fx.at[m], fx.at[m], lsem.at[L_FOUT + m]).wait()
-        send(S_FSIB + m, out_ag.at[f_row(m)], out_ag.at[f_row(m)], sibling)
+        send(S_FSIB + m, og.at[f_row(m)], og.at[f_row(m)], sibling)
+        local(L_AG + m, og.at[f_row(m)], out_ag.at[f_row(m)])
 
     shard_z = (z + y) % nz
     take(S_DT, dt_all.at[pl.ds(1, nx - 1)])
@@ -467,8 +480,12 @@
     u_new[...] = jnp.reshape(uag[...], (rank, cols))
     u_copy = local(L_U, u_new, out_u)
     for m in range(hx):
-        take(S_FSIB + m, out_ag.at[0])
-
+        take(S_FSIB + m, og.at[0])
+        row = (x + nx - (nx - 1 - own(m))) % nx
+        local(L_AG + hx + m, og.at[row], out_ag.at[row])
+
+    for m in range(2 * hx):
+        pltpu.make_async_copy(og.at[0], og.at[0], lsem.at[L_AG + m]).wait()
     out_copy.wait()
     d_copy.wait()
     u_copy.wait()
@@ -491,7 +508,7 @@
     for m in range(hx):
         sent(S_HSIB + m, h_sib.at[m])
         sent(S_HRS + m, hr.at[m, pl.ds(1, ny - 1)])
-        sent(S_FSIB + m, out_ag.at[0])
+        sent(S_FSIB + m, og.at[0])
 
     @pl.when(c != 0)
     def _():
@@ -502,6 +519,25 @@
     sent(S_ORS, o_recv.at[pl.ds(1, nz - 1)])
     sent(S_DX, d_recv.at[pl.ds(1, nx - 1)])
     sent(S_GG, gg_recv.at[pl.ds(1, ntp - 1)])
+
+
+def hand_over(*refs):
+    n = len(refs) // 3
+    srcs, dsts, held, into, out_of = refs[:n], refs[n:2 * n], refs[2 * n:3 * n], refs[-2], refs[-1]
+    ins, outs = [], []
+    for src, dst, mid in zip(srcs, dsts, held):
+        pieces = src.shape[0] if len(src.shape) == 4 else 1
+        for piece in range(pieces):
+            at = pl.ds(piece, 1) if pieces > 1 else slice(None)
+            ins.append(pltpu.make_async_copy(src.at[at], mid.at[at], into.at[len(ins)]))
+            outs.append(pltpu.make_async_copy(mid.at[at], dst.at[at], out_of.at[len(outs)]))
+    for copy in ins:
+        copy.start()
+    for copy, onward in zip(ins, outs):
+        copy.wait()
+        onward.start()
+    for copy in outs:
+        copy.wait()
 
 
 def body(residual, attention, codes, absmax, down, up, gate, selected, counts, cotangent,
@@ -539,7 +575,7 @@
             f32(rank, slots), f32(rank, slots), f32(ny, rank // ny, slots), f32(ny, rank // ny, slots),
             f32(rank // ny, slots), f32(ny, rank // ny, slots),
             bf16(nx, nz, cap, heads), bf16(hx, nz, cap, heads), bf16(hx, nz, cap, heads),
-            bf16(hx, ny, cap, heads), bf16(hx, cap, heads), bf16(hx, cap, heads),
+            bf16(hx, ny, cap, heads), bf16(hx, cap, heads), bf16(hx, cap, heads), bf16(nx, nz, cap, heads),
             f32(nz, rank // nz, cols), f32(nz, rank // nz, cols), f32(rank // nz, cols),
             f32(nx, rank // nz, cols), f32(nz, rank // nz, cols),
             bf16(nz, cap, cols), bf16(nz, cap, cols), f32(cap, cols), bf16(tokens, cols),
@@ -553,7 +589,15 @@
         name="block_step",
     )(residual, attention, codes, absmax.T, down.T, up, gate.reshape(1, cap), selected.reshape(1, cap),
       counts.reshape(1, 1), cotangent)
-    new_res, head_grad, d_grad, u_grad, g_grad = outs
+    new_res, head_grad, d_grad, u_grad, g_grad = pl.pallas_call(
+        hand_over,
+        out_shape=[jax.ShapeDtypeStruct(out.shape, out.dtype) for out in outs],
+        in_specs=[anywhere] * 5,
+        out_specs=[anywhere] * 5,
+        scratch_shapes=[pltpu.VMEM(out.shape, out.dtype) for out in outs]
+        + [pltpu.SemaphoreType.DMA((nx + 4,))] * 2,
+        name="hand_over",
+    )(*outs)
     return new_res, head_grad.reshape(nx * nz * cap, heads), d_grad.T, u_grad, g_grad.reshape(cap)
 
 

time: 66.6 us -> 62.6 us (0.940)
  local copies, waits for them, and re-layouts: 5.81 us -> 0 us
  Pallas kernels: 59.2 us -> 61.1 us
    unnamed x11 -> x0, local copies, waits for them, and re-layouts: 5.81 us -> none
    pallas_call x0 -> x1, Pallas kernels: none -> 2.17 us  [body(): pl.pallas_call(hand_over, out_shape=[jax.ShapeDtypeStruct(out.shape, out....]
where the time goes in v5:
time: 62.6 us; the launch traced here: 62.4 us
  Pallas kernels  61.1 us (98%)
  between operations  1.29 us (2%)
    pallas_call x1, Pallas kernels, body(): pl.pallas_call(functools.partial(kernel, nx, nz, ny), out_shape=(jax.Shap...  58.9 us
    pallas_call x1, Pallas kernels, body(): pl.pallas_call(hand_over, out_shape=[jax.ShapeDtypeStruct(out.shape, out....  2.17 us

profile of v5, /device:TPU:1, one launch (start us, length us, event | category | flops | bytes accessed | tf_op | source)
XLA Modules:
  0.0 62.4 jit_solution(9068385015975642143)
XLA Ops:
  1.3 58.9 %block_step.1 = (bf16[192,512]{1,0:T(8,128)(2,1)}, bf16[4,8,48,256]{3,2,1,0:T(8,128)(2,1)}, f32[64,256]{1,0:T(8,128)}, f32[64,512]{1,0:T(8,128)}, f32[1,48]{1,0:T(1,128)}) custom-call(bf16[192,512]{1,0:T(8,128)(2,1)} %res_hbm.1, bf16[48,8192]{1,0:T(8,128)(2,1)} %attn.1, s32[256,512]{1,0:T(8,128)} %codes_hbm.1, f32[8,256]{1,0:T(8,128)} %bitcast.10, ...), custom_call_target="tpu_custom_call" | custom-call | tf_op jit(solution)/shard_map/block_step/pallas_call | solution.py:560
  60.2 2.2 %hand_over.1 = (bf16[192,512]{1,0:T(8,128)(2,1)}, bf16[4,8,48,256]{3,2,1,0:T(8,128)(2,1)}, f32[64,256]{1,0:T(8,128)}, f32[64,512]{1,0:T(8,128)}, f32[1,48]{1,0:T(1,128)}) custom-call(bf16[192,512]{1,0:T(8,128)(2,1)} %get-tuple-element.15.refs_0_, bf16[4,8,48,256]{3,2,1,0:T(8,128)(2,1)} %get-tuple-element.16.refs_1_, f32[64,256]{1,0:T(8,128)} %get-tuple-element.17.refs_2_, ...), custom_call_target="tpu_custom_call" | custom-call | tf_op jit(solution)/shard_map/hand_over/pallas_call | solution.py:592

commit v6 on v5

--- a/solution.py
+++ b/solution.py
@@ -34,7 +34,7 @@
 (S_G, S_A, S_F0, S_F1, S_AZ, S_W1A, S_W1B, S_W3A, S_W3B, S_W2, S_DT, S_ASIB, S_RSIB, S_RRS, S_RAG,
  S_HSIB, S_HRS, S_FX, S_FSIB, S_URS, S_UX, S_UAG, S_ORS, S_DX, S_GG, N_SEM) = (
     0, 5, 10, 15, 20, *range(22, 32), 32, 34, 36, 38, *range(40, 47))
-DIRECT = (S_A,)
+DIRECT = (S_A, S_F0, S_F1)
 (L_COT, L_CODES, L_ABS, L_DOWN, L_UP, L_RES, L_A, L_OUT, L_D, L_U, L_FOUT, L_AG, N_LOC) = (*range(11), 12, 16)
 
 
@@ -63,7 +63,7 @@
            res, codes, absm, up, cot, scales,
            a_all, w_all, dt_all, g_all,
            rt, rt_sib, rt_send, rt_recv, rag_send, rag,
-           h_send, h_sib, hs, hr, f_send, fx, og,
+           h_send, h_sib, hs, hr, fx, og,
            u_send, u_recv, ux_send, ux_recv, uag,
            o_send, o_recv, o_home, new_res,
            d_send, d_recv, d_new, u_new, gg_send, gg_recv,
@@ -300,6 +300,8 @@
 
     up_in.wait()
     gather_finish(S_G, nz, g_like)
+    rt[...] = adapter_scale * dot(up[...], g_all[...], 1, 1)
+    send(S_RSIB, rt, rt_sib, sibling)
     rank_part = (adapter_scale * dot(g_all[...], up[...], 1, 1)).astype(BF16)
 
     def head_block(i):
@@ -314,33 +316,35 @@
         take(S_HSIB + m, h_sib.at[m])
         for j in range(nz):
             hs[m, j] = (h_send[own(m), j].astype(F32) + h_sib[m, j].astype(F32)).astype(BF16)
-        for k in range(1, ny):
-            send(S_HRS + m, hs.at[m, (y + k) % ny], hr.at[m, ny - k], dev_y(k))
-
-    def head_home(m):
-        take(S_HRS + m, hr.at[m, pl.ds(1, ny - 1)])
-        total = hs[m, y].astype(F32)
-        for k in range(1, ny):
-            total = total + hr[m, k].astype(F32)
-        f_send[m] = total.astype(BF16)
+        near = ((x + own(m)) % nx) * nz + z
+        for k in (4, 3, 5, 2, 6, 1, 7) if ny == 8 else range(1, ny):
+            send(S_HRS + m, hs.at[m, (y + k) % ny], hr.at[m, ny - k], (near, ((y + k) % ny) * NC + c))
         if m == 0:
             @pl.when(c == 0)
             def _():
-                fx[0] = f_send[0]
+                hr[0, 0] = hs[0, y]
 
             @pl.when(c != 0)
             def _():
-                send(S_FX, f_send.at[0], fx.at[0], dev_x(nx - 1))
+                send(S_HRS, hs.at[0, y], hr.at[0, 0], (near, tp))
         else:
-            send(S_FX + m, f_send.at[m], fx.at[m], dev_x(own(m)))
-
-    def head_gather(m):
+            send(S_HRS + m, hs.at[m, y], hr.at[m, 0], (near, tp))
+
+    def head_home(m):
         if m == 0:
+            @pl.when(c == 0)
+            def _():
+                take(S_HRS, hr.at[0, pl.ds(1, ny - 1)])
+
             @pl.when(c != 0)
             def _():
-                take(S_FX, fx.at[0])
+                take(S_HRS, hr.at[0])
         else:
-            take(S_FX + m, fx.at[m])
+            take(S_HRS + m, hr.at[m])
+        total = hr[m, 0].astype(F32)
+        for k in range(1, ny):
+            total = total + hr[m, k].astype(F32)
+        fx[m] = total.astype(BF16)
         local(L_FOUT + m, fx.at[m], og.at[f_row(m), shard_z])
         gather_start(S_F0 + 5 * m, ny, dev_y, f_parts(m))
 
@@ -359,8 +363,12 @@
     take(S_W3B, half_w)
     head_block(3)
     head_pair(0)
-    rt[...] = adapter_scale * dot(up[...], g_all[...], 1, 1)
-    send(S_RSIB, rt, rt_sib, sibling)
+    take(S_RSIB, rt_sib)
+    for j in range(ny):
+        rows = pl.ds(j * (rank // ny), rank // ny)
+        rt_send[j] = rt[rows, :] + rt_sib[rows, :]
+    for k in range(1, ny):
+        send(S_RRS, rt_send.at[(y + k) % ny], rt_recv.at[ny - k], dev_y(k))
     take(S_W1B, half_w)
     head_block(1)
     head_sum(0)
@@ -370,13 +378,16 @@
     gather_finish(S_A, ny, a_like)
     a_mine = a_all.at[pl.ds(hx * c, hx)]
     send(S_ASIB, a_mine, a_mine, sibling)
-    take(S_RSIB, rt_sib)
-    for j in range(ny):
-        rows = pl.ds(j * (rank // ny), rank // ny)
-        rt_send[j] = rt[rows, :] + rt_sib[rows, :]
+    head_sum(1)
+    take(S_RRS, rt_recv.at[pl.ds(1, ny - 1)])
+    total = rt_send[y]
     for k in range(1, ny):
-        send(S_RRS, rt_send.at[(y + k) % ny], rt_recv.at[ny - k], dev_y(k))
-    head_sum(1)
+        total = total + rt_recv[k]
+    rag_send[...] = total.astype(BF16).astype(F32)
+    rag[y] = rag_send[...]
+    for k in range(1, ny):
+        send(S_RAG, rag_send, rag.at[y], dev_y(k))
+
 
     take(S_ASIB, a_mine)
     low = jnp.zeros((slots, rank), F32)
@@ -401,28 +412,7 @@
     for k in range(1, nz):
         send(S_ORS, o_send.at[k], o_recv.at[nz - k], dev_z(k))
 
-    take(S_RRS, rt_recv.at[pl.ds(1, ny - 1)])
-    total = rt_send[y]
-    for k in range(1, ny):
-        total = total + rt_recv[k]
-    rag_send[...] = total.astype(BF16).astype(F32)
-    rag[y] = rag_send[...]
-    for k in range(1, ny):
-        send(S_RAG, rag_send, rag.at[y], dev_y(k))
-
     head_home(0)
-    head_home(1)
-    head_gather(0)
-
-    take(S_RAG, rag.at[pl.ds(0, ny - 1)])
-    full_rt = jnp.reshape(rag[...], (rank, slots)).astype(BF16)
-    for i in range(nx):
-        d_send[i] = dot(full_rt, a_all[i], 1, 0)
-    for k in range(1, nx):
-        send(S_DX, d_send.at[k], d_recv.at[nx - k], dev_x(k))
-    head_gather(1)
-    head_forward(0)
-
     take(S_URS, u_recv.at[pl.ds(1, nz - 1)])
     total = u_send[z]
     for k in range(1, nz):
@@ -430,6 +420,16 @@
     ux_send[...] = total
     for k in range(1, nx):
         send(S_UX, ux_send, ux_recv.at[nx - k], dev_x(k))
+
+    head_home(1)
+
+    take(S_RAG, rag.at[pl.ds(0, ny - 1)])
+    full_rt = jnp.reshape(rag[...], (rank, slots)).astype(BF16)
+    for i in range(nx):
+        d_send[i] = dot(full_rt, a_all[i], 1, 0)
+    for k in range(1, nx):
+        send(S_DX, d_send.at[k], d_recv.at[nx - k], dev_x(k))
+    head_forward(0)
 
     head_forward(1)
     take(S_ORS, o_recv.at[pl.ds(1, nz - 1)])
@@ -507,13 +507,16 @@
     sent(S_RAG, rag.at[pl.ds(0, ny - 1)])
     for m in range(hx):
         sent(S_HSIB + m, h_sib.at[m])
-        sent(S_HRS + m, hr.at[m, pl.ds(1, ny - 1)])
         sent(S_FSIB + m, og.at[0])
+
+    @pl.when(c == 0)
+    def _():
+        sent(S_HRS, hr.at[0, pl.ds(1, ny - 1)])
 
     @pl.when(c != 0)
     def _():
-        sent(S_FX, fx.at[0])
-    sent(S_FX + 1, fx.at[1])
+        sent(S_HRS, hr.at[0])
+    sent(S_HRS + 1, hr.at[1])
     sent(S_URS, u_recv.at[pl.ds(1, nz - 1)])
     sent(S_UAG, uag.at[pl.ds(0, nz - 1)])
     sent(S_ORS, o_recv.at[pl.ds(1, nz - 1)])
@@ -575,7 +578,7 @@
             f32(rank, slots), f32(rank, slots), f32(ny, rank // ny, slots), f32(ny, rank // ny, slots),
             f32(rank // ny, slots), f32(ny, rank // ny, slots),
             bf16(nx, nz, cap, heads), bf16(hx, nz, cap, heads), bf16(hx, nz, cap, heads),
-            bf16(hx, ny, cap, heads), bf16(hx, cap, heads), bf16(hx, cap, heads), bf16(nx, nz, cap, heads),
+            bf16(hx, ny, cap, heads), bf16(hx, cap, heads), bf16(nx, nz, cap, heads),
             f32(nz, rank // nz, cols), f32(nz, rank // nz, cols), f32(rank // nz, cols),
             f32(nx, rank // nz, cols), f32(nz, rank // nz, cols),
             bf16(nz, cap, cols), bf16(nz, cap, cols), f32(cap, cols), bf16(tokens, cols),

time: 62.6 us -> 60.2 us (0.962)
  Pallas kernels: 61.1 us -> 58.3 us
    pallas_call x1, Pallas kernels: 58.9 us -> 56.2 us  [body(): pl.pallas_call(functools.partial(kernel, nx, nz, ny), out_shape=(jax.Shap...]
where the time goes in v6:
time: 60.2 us; the launch traced here: 59.6 us
  Pallas kernels  58.3 us (97%)
  between operations  1.29 us (2%)
    pallas_call x1, Pallas kernels, body(): pl.pallas_call(functools.partial(kernel, nx, nz, ny), out_shape=(jax.Shap...  56.2 us
    pallas_call x1, Pallas kernels, body(): pl.pallas_call(hand_over, out_shape=[jax.ShapeDtypeStruct(out.shape, out....  2.17 us

profile of v6, /device:TPU:1, one launch (start us, length us, event | category | flops | bytes accessed | tf_op | source)
XLA Modules:
  0.0 59.6 jit_solution(18357167129555941421)
XLA Ops:
  1.3 56.2 %block_step.1 = (bf16[192,512]{1,0:T(8,128)(2,1)}, bf16[4,8,48,256]{3,2,1,0:T(8,128)(2,1)}, f32[64,256]{1,0:T(8,128)}, f32[64,512]{1,0:T(8,128)}, f32[1,48]{1,0:T(1,128)}) custom-call(bf16[192,512]{1,0:T(8,128)(2,1)} %res_hbm.1, bf16[48,8192]{1,0:T(8,128)(2,1)} %attn.1, s32[256,512]{1,0:T(8,128)} %codes_hbm.1, f32[8,256]{1,0:T(8,128)} %bitcast.10, ...), custom_call_target="tpu_custom_call" | custom-call | tf_op jit(solution)/shard_map/block_step/pallas_call | solution.py:563
  57.5 2.2 %hand_over.1 = (bf16[192,512]{1,0:T(8,128)(2,1)}, bf16[4,8,48,256]{3,2,1,0:T(8,128)(2,1)}, f32[64,256]{1,0:T(8,128)}, f32[64,512]{1,0:T(8,128)}, f32[1,48]{1,0:T(1,128)}) custom-call(bf16[192,512]{1,0:T(8,128)(2,1)} %get-tuple-element.15.refs_0_, bf16[4,8,48,256]{3,2,1,0:T(8,128)(2,1)} %get-tuple-element.16.refs_1_, f32[64,256]{1,0:T(8,128)} %get-tuple-element.17.refs_2_, ...), custom_call_target="tpu_custom_call" | custom-call | tf_op jit(solution)/shard_map/hand_over/pallas_call | solution.py:595

commit v7 on v6

--- a/solution.py
+++ b/solution.py
@@ -449,6 +449,7 @@
     new_res[...] = jnp.where(taken, spread, res[...].astype(F32)).astype(BF16)
     out_copy = local(L_OUT, new_res, out_res)
 
+    head_finish(0)
     take(S_UX, ux_recv.at[pl.ds(1, nx - 1)])
     total = ux_send[...]
     for k in range(1, nx):
@@ -467,8 +468,7 @@
     d_new[...] = total
     d_copy = local(L_D, d_new, out_d)
 
-    for m in range(hx):
-        head_finish(m)
+    head_finish(1)
 
     take(S_GG, gg_recv.at[pl.ds(1, ntp - 1)])
     total = gg_send[...]

time: 60.2 us -> 60.3 us (level)
  no operation moved by 1% of the time
where the time goes in v7:
time: 60.3 us; the launch traced here: 59.6 us
  Pallas kernels  58.3 us (97%)
  between operations  1.29 us (2%)
    pallas_call x1, Pallas kernels, body(): pl.pallas_call(functools.partial(kernel, nx, nz, ny), out_shape=(jax.Shap...  56.2 us
    pallas_call x1, Pallas kernels, body(): pl.pallas_call(hand_over, out_shape=[jax.ShapeDtypeStruct(out.shape, out....  2.17 us

profile of v7, /device:TPU:1, one launch (start us, length us, event | category | flops | bytes accessed | tf_op | source)
XLA Modules:
  0.0 59.6 jit_solution(5504904757676056345)
XLA Ops:
  1.3 56.2 %block_step.1 = (bf16[192,512]{1,0:T(8,128)(2,1)}, bf16[4,8,48,256]{3,2,1,0:T(8,128)(2,1)}, f32[64,256]{1,0:T(8,128)}, f32[64,512]{1,0:T(8,128)}, f32[1,48]{1,0:T(1,128)}) custom-call(bf16[192,512]{1,0:T(8,128)(2,1)} %res_hbm.1, bf16[48,8192]{1,0:T(8,128)(2,1)} %attn.1, s32[256,512]{1,0:T(8,128)} %codes_hbm.1, f32[8,256]{1,0:T(8,128)} %bitcast.10, ...), custom_call_target="tpu_custom_call" | custom-call | tf_op jit(solution)/shard_map/block_step/pallas_call | solution.py:563
  57.5 2.2 %hand_over.1 = (bf16[192,512]{1,0:T(8,128)(2,1)}, bf16[4,8,48,256]{3,2,1,0:T(8,128)(2,1)}, f32[64,256]{1,0:T(8,128)}, f32[64,512]{1,0:T(8,128)}, f32[1,48]{1,0:T(1,128)}) custom-call(bf16[192,512]{1,0:T(8,128)(2,1)} %get-tuple-element.15.refs_0_, bf16[4,8,48,256]{3,2,1,0:T(8,128)(2,1)} %get-tuple-element.16.refs_1_, f32[64,256]{1,0:T(8,128)} %get-tuple-element.17.refs_2_, ...), custom_call_target="tpu_custom_call" | custom-call | tf_op jit(solution)/shard_map/hand_over/pallas_call | solution.py:595
